TPU v7x, 32 devices: a whole 2x2x4 slice. The times are simulated.
32 devices in a mesh: comp: 2 (over core), gx: 4 (over y, x), gy: 4 (over z).
Axes of the slice: x: 2, y: 2, z: 4, core: 2. Of those that a mesh axis runs over, the one named last changes fastest.
Arguments:
- state: float32 [2, 8, 96, 3072], P('comp', None, 'gx', 'gy'), may hold values from -6 to 6
- response: float32 [2, 8, 3072], P('comp'), may hold values from -0.95 to 0
- diffusion: float32 [2, 96, 3072], P('comp', 'gx', 'gy'), may hold values from 0.02 to 0.24
- land_mask: int32 [96, 3072], P('gx', 'gy'), may hold values 0 or 1
- couple_src: int32 [2, 4, 4, 16, 128], P('comp', 'gx', 'gy'), may hold values from 0 to 18431
- couple_dst: int32 [2, 4, 4, 16, 128], P('comp', 'gx', 'gy'), may hold values from 0 to 18431
- couple_weight: float32 [2, 4, 4, 16, 128], P('comp', 'gx', 'gy'), may hold values from 0.1 to 1
- couple_count: int32 [2, 4, 4, 16], P('comp', 'gx', 'gy'), may hold values from 0 to 128, as said below
Outputs:
- final_state: float32 [2, 8, 96, 3072], P('comp', None, 'gx', 'gy')
Inputs may be any that keep to these rules, and one draw needn't show every extreme that they name: `couple_count`: at most 128 live slots per ordered device pair; every sending device has one pair with exactly 128.
All inputs are finite; a program needn't handle non-finite values. No bound on the sum of `land_mask` on one device may be relied on, other than what follows from the above.
Results may differ from a plain program's by a relative error of at most 0.0095.
Values may be sent and summed in bfloat16 or wider, within the bound.
A program may use at most 128 MiB of HBM per device.

v0:
```python
import math

import jax
import jax.numpy as jnp
from jax import lax
from jax.sharding import PartitionSpec as P

FC = 4


def extended(block, sides, width):
    for axis, dim in sides:
        count = lax.axis_size(axis)
        forward = [(i, i + 1) for i in range(count - 1)]
        backward = [(target, source) for source, target in forward]
        low = lax.ppermute(
            lax.slice_in_dim(block, block.shape[dim] - width, None, axis=dim), axis, forward
        )
        high = lax.ppermute(lax.slice_in_dim(block, 0, width, axis=dim), axis, backward)
        block = jnp.concatenate([low, block, high], axis=dim)
    return block


def partner(value, axis, stride):
    mask = 2**stride
    pairs = [(source, source ^ mask) for source in range(lax.axis_size(axis))]
    return lax.ppermute(value, axis, pairs)


def make_table(cols):
    rows_idx = jnp.arange(cols, dtype=jnp.int32)[:, None]
    wave_idx = jnp.arange(cols // 2, dtype=jnp.int32)[None, :]
    phase = rows_idx * wave_idx % cols
    angle = phase.astype(jnp.float32) * (2.0 * math.pi / cols)
    return jnp.concatenate([jnp.cos(angle), jnp.sin(angle)], axis=1).astype(jnp.bfloat16)


def back_transform(filtered, table_part):
    return lax.dot_general(
        filtered, table_part, (((1,), (1,)), ((), ())), preferred_element_type=jnp.float32
    )


def circle_increment(circles, resp_part, table, scale):
    count, rows_part, cols_all = circles.shape
    spec = jnp.dot(circles.reshape(-1, cols_all), table, preferred_element_type=jnp.float32)
    spec = spec.reshape(count, rows_part, cols_all)
    filtered = (spec * resp_part[:, None, :]).astype(jnp.bfloat16)
    incr = (back_transform(filtered.reshape(-1, cols_all), table) * scale).astype(jnp.bfloat16)
    return incr.reshape(count, rows_part, cols_all)


def diffuse(fields, rate):
    padded = extended(fields.astype(jnp.bfloat16), (("gx", 1),), 1).astype(fields.dtype)
    return fields + rate[None] * (padded[:, 2:] + padded[:, :-2] - 2.0 * fields)


def local(
    state, response, diffusion, land_mask, couple_src, couple_dst, couple_weight, couple_count
):
    levels, rows_dev, cols_dev = (state.shape[1], state.shape[2], state.shape[3])
    groups_x = lax.axis_size("gx")
    groups_y = lax.axis_size("gy")
    peers = groups_x * groups_y
    slots = couple_src.shape[4]
    cells = rows_dev * cols_dev
    cols_all = cols_dev * groups_y
    per_level = levels // groups_y
    section = lax.axis_index("comp")
    keep = jnp.where(section == 1, land_mask.astype(jnp.float32), jnp.float32(1.0))
    table = make_table(cols_all)
    scale = 2.0 / cols_all
    src_idx = couple_src.reshape(peers, slots)
    dst_idx = couple_dst.reshape(peers, slots)
    live = jnp.arange(slots, dtype=jnp.int32)[None, :] < couple_count.reshape(peers, 1)
    weights = jnp.where(live, couple_weight.reshape(peers, slots), jnp.float32(0.0))
    first_level = lax.axis_index("gy") * per_level
    resp_mine = lax.dynamic_slice_in_dim(response[0], first_level, per_level, 0)
    rate = diffusion[0]
    fields = state[0]
    surface = fields[:FC].reshape(FC, cells)
    outgoing = jnp.transpose(surface[:, src_idx] * weights[None], (1, 0, 2))
    crossed = partner(outgoing, "comp", 0)
    arrived = lax.all_to_all(crossed, ("gx", "gy"), split_axis=0, concat_axis=0, tiled=True)
    incoming = jnp.transpose(arrived, (1, 0, 2))
    surface = surface.at[:, dst_idx].add(incoming)
    surf = surface.reshape(FC, rows_dev, cols_dev)
    fields = jnp.concatenate([surf, fields[FC:]], axis=0)
    grid_bf = fields.astype(jnp.bfloat16)
    circles = lax.all_to_all(grid_bf, "gy", split_axis=0, concat_axis=2, tiled=True)
    incr = circle_increment(circles, resp_mine, table, scale)
    incr = lax.all_to_all(incr, "gy", split_axis=2, concat_axis=0, tiled=True)
    fields = fields + incr.astype(jnp.float32)
    fields = diffuse(fields, rate) * keep[None]
    return fields[None]


def solution(mesh):
    return jax.shard_map(
        local,
        mesh=mesh,
        in_specs=(
            P("comp", None, "gx", "gy"),
            P("comp", None, None),
            P("comp", "gx", "gy"),
            P("gx", "gy"),
            P("comp", "gx", "gy", None, None),
            P("comp", "gx", "gy", None, None),
            P("comp", "gx", "gy", None, None),
            P("comp", "gx", "gy", None),
        ),
        out_specs=P("comp", None, "gx", "gy"),
        check_vma=False,
    )
```

profile of v0, /device:TPU:0, one launch (start us, length us, event | category | flops | bytes accessed | tf_op | source)
XLA Modules:
  0.0 197.7 jit_solution(5701691548152781341)
XLA Ops:
  0.0 0.0 copy-start
  0.0 0.0 copy-start.2
  0.0 0.0 copy-start.3
  0.0 0.0 copy-start.5
  0.0 0.0 copy-start.4
  0.0 1.1 fusion.28
  1.1 0.0 copy-start.1
  1.2 5.6 %copy.20 = f32[1,4,24,768]{1,3,2,0:T(8,128)} copy(f32[1,4,24,768]{3,2,1,0:T(8,128)S(1)} %get-tuple-element.5) | data formatting | bytes 589824 | tf_op jit(solution)/shard_map/slice | solution.py:81
  6.8 0.0 copy-done.2
  6.8 9.1 %gather_fusion = f32[2048,4]{1,0:T(8,128)S(1)} fusion(f32[4,18432]{0,1:T(8,128)} %bitcast.55, s32[2048]{0:T(1024)S(1)} %fusion.25), kind=kCustom, calls=%fused_computation | custom fusion | bytes 73728 | tf_op jit(solution)/shard_map/gather | solution.py:82
  15.9 0.3 copy.21
  16.3 0.0 copy-done.3
  16.3 0.0 copy-done.5
  16.3 0.1 bitcast_select_fusion
  16.4 0.6 collective-permute-start
  17.0 0.9 collective-permute-done
  17.8 0.6 copy.22
  18.5 8.2 %all-to-all-start = ((f32[16,4,128]{2,1,0:T(4,128)}), f32[16,4,128]{2,1,0:T(4,128)S(1)}, u32[]{:S(2)}, u32[]{:S(2)}) async-start(f32[16,4,128]{2,1,0:T(4,128)} %copy.22), calls=%async_computation | async-start | bytes 65536 | tf_op jit(solution)/shard_map/all_to_all | solution.py:84
  26.7 0.0 copy-done.4
  26.7 7.3 %all-to-all-done = f32[16,4,128]{2,1,0:T(4,128)S(1)} async-done(((f32[16,4,128]{2,1,0:T(4,128)}), f32[16,4,128]{2,1,0:T(4,128)S(1)}, u32[]{:S(2)}, u32[]{:S(2)}) %all-to-all-start) | async-done | bytes 32800 | tf_op jit(solution)/shard_map/all_to_all | solution.py:84
  34.0 0.4 copy.23
  34.4 17.6 %scatter_fusion = f32[4,18432]{0,1:T(8,128)} fusion(f32[4,18432]{0,1:T(8,128)} %bitcast.56, s32[2048]{0:T(1024)S(1)} %fusion.23, f32[2048,4]{1,0:T(8,128)S(1)} %copy.23), kind=kCustom, calls=%fused_computation.1 | custom fusion | flops 8192 | bytes 106496 | tf_op jit(solution)/shard_map/scatter-add | solution.py:86
  52.0 6.4 %copy.24 = f32[4,24,768]{2,1,0:T(8,128)S(1)} copy(f32[4,24,768]{0,2,1:T(8,128)} %bitcast.57) | data formatting | bytes 589824 | tf_op jit(solution)/shard_map/reshape | solution.py:87
  58.4 0.0 copy-done.1
  58.4 0.7 fusion.21
  59.2 3.5 %all-to-all-start.1 = ((bf16[8,24,768]{2,1,0:T(8,128)(2,1)}), bf16[8,24,768]{2,1,0:T(8,128)(2,1)S(1)}, u32[]{:S(2)}, u32[]{:S(2)}) async-start(bf16[8,24,768]{2,1,0:T(8,128)(2,1)} %fusion.21), calls=%async_computation.1 | async-start | bytes 589824 | tf_op jit(solution)/shard_map/all_to_all | solution.py:90
  62.6 79.5 %sine_convert_fusion = (bf16[3072,1536]{1,0:T(8,128)(2,1)}, bf16[3072,1536]{1,0:T(8,128)(2,1)}) fusion(), kind=kLoop, calls=%fused_computation.8 | loop fusion | flops 51904512 | bytes 18874368 | tf_op jit(solution)/shard_map/convert.4
  142.2 0.0 copy-done
  142.2 0.0 all-to-all-done.1
  142.2 0.2 copy.29
  142.4 0.2 dot_general.8
  142.6 8.2 %fusion.12 = bf16[2,24,3072]{2,1,0:T(8,128)(2,1)S(1)} fusion(bf16[2,24,3072]{2,1,0:T(8,128)(2,1)S(1)} %dot_general.8, bf16[3072,1536]{1,0:T(8,128)(2,1)} %get-tuple-element.9, bf16[3072,1536]{1,0:T(8,128)(2,1)} %get-tuple-element.10, f32[2,3072]{1,0:T(2,128)S(1)} %dynamic-slice_bitcast_fusion), kind=kOutput, calls=%fused_computation.17 | convolution fusion | flops 944013312 | bytes 19488768 | tf_op jit(solution)/shard_map/dot_general | solution.py:46
  150.8 9.6 %fusion.15 = bf16[48,3072]{1,0:T(8,128)(2,1)S(1)} fusion(bf16[48,3072]{1,0:T(8,128)(2,1)S(1)} %bitcast.67, bf16[3072,1536]{1,0:T(8,128)(2,1)} %get-tuple-element.9, bf16[3072,1536]{1,0:T(8,128)(2,1)} %get-tuple-element.10), kind=kOutput, calls=%fused_computation.18 | convolution fusion | flops 944013312 | bytes 19464192 | tf_op jit(solution)/shard_map/dot_general | solution.py:39
  160.4 1.9 copy.26
  162.3 2.6 %reshape.148 = bf16[4,2,18432]{2,1,0:T(2,128)(2,1)} reshape(bf16[3072,2,24]{2,1,0:T(2,128)(2,1)S(1)} %bitcast.58) | data formatting | bytes 589824
  165.0 5.1 %all-to-all-start.2 = ((bf16[4,2,18432]{2,1,0:T(2,128)(2,1)}), bf16[4,2,18432]{2,1,0:T(2,128)(2,1)S(1)}, u32[]{:S(2)}, u32[]{:S(2)}) async-start(bf16[4,2,18432]{2,1,0:T(2,128)(2,1)} %reshape.148), calls=%async_computation.2 | async-start | bytes 589824 | tf_op jit(solution)/shard_map/all_to_all | solution.py:92
  170.0 8.3 %all-to-all-done.2 = bf16[4,2,18432]{2,1,0:T(2,128)(2,1)S(1)} async-done(((bf16[4,2,18432]{2,1,0:T(2,128)(2,1)}), bf16[4,2,18432]{2,1,0:T(2,128)(2,1)S(1)}, u32[]{:S(2)}, u32[]{:S(2)}) %all-to-all-start.2) | async-done | bytes 294944 | tf_op jit(solution)/shard_map/all_to_all | solution.py:92
  178.3 3.1 %reshape.149 = bf16[3072,2,24]{2,1,0:T(2,128)(2,1)} reshape(bf16[4,2,18432]{2,1,0:T(2,128)(2,1)S(1)} %all-to-all-done.2) | data formatting | bytes 589824
  181.4 2.5 %convert_bitcast_fusion = f32[4,2,24,768]{2,1,3,0:T(2,128)S(1)} fusion(bf16[2,24,4,768]{1,0,3,2:T(2,128)(2,1)} %bitcast.59), kind=kLoop, calls=%fused_computation.19 | loop fusion | flops 147456 | bytes 884736 | tf_op jit(solution)/shard_map/convert_element_type | solution.py:93
  183.9 2.8 %copy.27 = f32[4,2,24,768]{3,2,1,0:T(8,128)} copy(f32[4,2,24,768]{2,1,3,0:T(2,128)S(1)} %convert_bitcast_fusion) | data formatting | bytes 1179648 | tf_op jit(solution)/shard_map/convert_element_type | solution.py:93
  186.8 1.2 fusion.22
  188.0 1.3 collective-permute-start.2
  189.3 4.5 %collective-permute-start.1 = (bf16[8,1,768]{2,1,0:T(2,128)(2,1)S(1)}, bf16[8,1,768]{2,1,0:T(2,128)(2,1)S(1)}, u32[]{:S(2)}, u32[]{:S(2)}) collective-permute-start(bf16[8,1,768]{2,1,0:T(2,128)(2,1)S(1)} %get-tuple-element.7), channel_id=1, source_target_pairs={{0,4},{4,8},{8,12},{1,5},{5,9},{9,13},{2,6},{6,10},{10,14},{3,7},{... | collective-permute-start | bytes 36872 | tf_op jit(solution)/shard_map/ppermute | solution.py:16
  193.9 0.9 convert_select_fusion
  194.8 0.0 collective-permute-done.2
  194.8 0.6 collective-permute-done.1
  195.4 0.1 maximum_convert_fusion
  195.5 2.2 %fusion.20 = f32[1,8,24,768]{3,2,1,0:T(8,128)} fusion(f32[8,26,768]{2,1,0:T(8,128)S(1)} %maximum_convert_fusion, f32[24,768]{1,0:T(8,128)S(1)} %convert_select_fusion, f32[24,768]{1,0:T(8,128)} %bitcast.65, f32[4,2,24,768]{3,2,1,0:T(8,128)} %copy.27, f32[4,24,768]{2,1,0:T(8,128)} %copy-done.1, f32[4,24,768]{2,1,0:T(8,128)S(1)} %copy.24), kind=kLoop, calls=%fused_computation.25 | loop fusion | flops 1179648 | bytes 3096576 | tf_op jit(solution)/shard_map/broadcast_in_dim | solution.py:95
  (5 shorter events, 0.1 us)
Async XLA Ops:
  0.0 142.2 %copy-start = (f32[1,8,3072]{2,1,0:T(8,128)S(1)}, f32[1,8,3072]{2,1,0:T(8,128)}, u32[]{:S(2)}) copy-start(f32[1,8,3072]{2,1,0:T(8,128)} %param.9) | copy-start | bytes 294916
  0.0 6.8 %copy-start.2 = (s32[1,1,1,16,128]{4,3,2,1,0:T(8,128)S(1)}, s32[1,1,1,16,128]{4,3,2,1,0:T(8,128)}, u32[]{:S(2)}) copy-start(s32[1,1,1,16,128]{4,3,2,1,0:T(8,128)} %param.12) | copy-start | bytes 24580
  0.0 16.3 %copy-start.3 = (f32[1,1,1,16,128]{4,3,2,1,0:T(8,128)S(1)}, f32[1,1,1,16,128]{4,3,2,1,0:T(8,128)}, u32[]{:S(2)}) copy-start(f32[1,1,1,16,128]{4,3,2,1,0:T(8,128)} %param.14) | copy-start | bytes 24580
  0.0 16.3 %copy-start.5 = (s32[1,1,1,16]{3,2,1,0:T(1,128)S(1)}, s32[1,1,1,16]{3,2,1,0:T(1,128)}, u32[]{:S(2)}) copy-start(s32[1,1,1,16]{3,2,1,0:T(1,128)} %param.15) | copy-start | bytes 196
  0.0 26.6 %copy-start.4 = (s32[1,1,1,16,128]{4,3,2,1,0:T(8,128)S(1)}, s32[1,1,1,16,128]{4,3,2,1,0:T(8,128)}, u32[]{:S(2)}) copy-start(s32[1,1,1,16,128]{4,3,2,1,0:T(8,128)} %param.13) | copy-start | bytes 24580
  1.1 57.3 %copy-start.1 = (f32[4,24,768]{2,1,0:T(8,128)}, f32[4,24,768]{2,1,0:T(8,128)S(1)}, u32[]{:S(2)}) copy-start(f32[4,24,768]{2,1,0:T(8,128)S(1)} %get-tuple-element.6) | copy-start | bytes 884740
  16.4 1.4 collective-permute-start
  18.5 15.6 %all-to-all-start = ((f32[16,4,128]{2,1,0:T(4,128)}), f32[16,4,128]{2,1,0:T(4,128)S(1)}, u32[]{:S(2)}, u32[]{:S(2)}) async-start(f32[16,4,128]{2,1,0:T(4,128)} %copy.22), calls=%async_computation | async-start | bytes 65536 | tf_op jit(solution)/shard_map/all_to_all | solution.py:84
  59.2 83.0 %all-to-all-start.1 = ((bf16[8,24,768]{2,1,0:T(8,128)(2,1)}), bf16[8,24,768]{2,1,0:T(8,128)(2,1)S(1)}, u32[]{:S(2)}, u32[]{:S(2)}) async-start(bf16[8,24,768]{2,1,0:T(8,128)(2,1)} %fusion.21), calls=%async_computation.1 | async-start | bytes 589824 | tf_op jit(solution)/shard_map/all_to_all | solution.py:90
  165.0 13.3 %all-to-all-start.2 = ((bf16[4,2,18432]{2,1,0:T(2,128)(2,1)}), bf16[4,2,18432]{2,1,0:T(2,128)(2,1)S(1)}, u32[]{:S(2)}, u32[]{:S(2)}) async-start(bf16[4,2,18432]{2,1,0:T(2,128)(2,1)} %reshape.148), calls=%async_computation.2 | async-start | bytes 589824 | tf_op jit(solution)/shard_map/all_to_all | solution.py:92
  188.0 6.8 %collective-permute-start.2 = (bf16[8,1,768]{2,1,0:T(2,128)(2,1)S(1)}, bf16[8,1,768]{2,1,0:T(2,128)(2,1)S(1)}, u32[]{:S(2)}, u32[]{:S(2)}) collective-permute-start(bf16[8,1,768]{2,1,0:T(2,128)(2,1)S(1)} %get-tuple-element.8), channel_id=1, source_target_pairs={{4,0},{8,4},{12,8},{5,1},{9,5},{13,9},{6,2},{10,6},{14,10},{7,3},{... | collective-permute-start | bytes 36872 | tf_op jit(solution)/shard_map/ppermute | solution.py:19
  189.3 6.1 %collective-permute-start.1 = (bf16[8,1,768]{2,1,0:T(2,128)(2,1)S(1)}, bf16[8,1,768]{2,1,0:T(2,128)(2,1)S(1)}, u32[]{:S(2)}, u32[]{:S(2)}) collective-permute-start(bf16[8,1,768]{2,1,0:T(2,128)(2,1)S(1)} %get-tuple-element.7), channel_id=1, source_target_pairs={{0,4},{4,8},{8,12},{1,5},{5,9},{9,13},{2,6},{6,10},{10,14},{3,7},{... | collective-permute-start | bytes 36872 | tf_op jit(solution)/shard_map/ppermute | solution.py:16
where the time goes:
time: 199 us; the launch traced here: 198 us
  other arithmetic  105 us (53%)
  local copies, waits for them, and re-layouts  34.5 us (17%)
  starting transfers between devices  23.1 us (12%)
  matrix products  17.8 us (9%)
  waiting for transfers between devices  17.1 us (9%)
    another operation x1, other arithmetic  79.5 us
    scatter-add x1, other arithmetic, local(): surface = surface.at[:, dst_idx].add(incoming)  17.6 us
    dot_general x1, matrix products, back_transform(): lax.dot_general(filtered, table_part, (((1,), (1,)), ((), ())), preferred...  9.63 us
    gather x2, local copies, waits for them, and re-layouts, local(): outgoing = jnp.transpose(surface[:, src_idx] * weights[None], (1, 0, 2))  9.47 us
    all_to_all x1, waiting for transfers between devices, local(): incr = lax.all_to_all(incr, 'gy', split_axis=2, concat_axis=0, tiled=True)  8.3 us
    dot_general x1, matrix products, circle_increment(): jnp.dot(circles.reshape(-1, cols_all), table, preferred_element_type=jnp....  8.22 us
    all_to_all x1, starting transfers between devices, local(): lax.all_to_all(crossed, ('gx', 'gy'), split_axis=0, concat_axis=0, tiled=...  8.2 us
    all_to_all x1, waiting for transfers between devices, local(): lax.all_to_all(crossed, ('gx', 'gy'), split_axis=0, concat_axis=0, tiled=...  7.34 us
  transfers between devices with their start and end apart: 6, of which 4 were waited for; matrix products, arithmetic and copies ran while one was open for 41% of the time, Pallas kernels for 0%

commit v1 on v0

--- a/solution.py
+++ b/solution.py
@@ -28,11 +28,22 @@
 
 
 def make_table(cols):
-    rows_idx = jnp.arange(cols, dtype=jnp.int32)[:, None]
+    split = 64 if cols % 64 == 0 else 1
     wave_idx = jnp.arange(cols // 2, dtype=jnp.int32)[None, :]
-    phase = rows_idx * wave_idx % cols
-    angle = phase.astype(jnp.float32) * (2.0 * math.pi / cols)
-    return jnp.concatenate([jnp.cos(angle), jnp.sin(angle)], axis=1).astype(jnp.bfloat16)
+    scale = 2.0 * math.pi / cols
+
+    def trig(rows_idx):
+        angle = (rows_idx * wave_idx % cols).astype(jnp.float32) * scale
+        return jnp.cos(angle), jnp.sin(angle)
+
+    cos_hi, sin_hi = trig(jnp.arange(cols // split, dtype=jnp.int32)[:, None] * split)
+    cos_lo, sin_lo = trig(jnp.arange(split, dtype=jnp.int32)[:, None])
+    cos_hi, sin_hi = cos_hi[:, None], sin_hi[:, None]
+    cos_lo, sin_lo = cos_lo[None], sin_lo[None]
+    cos_all = cos_hi * cos_lo - sin_hi * sin_lo
+    sin_all = sin_hi * cos_lo + cos_hi * sin_lo
+    table = jnp.concatenate([cos_all, sin_all], axis=2).astype(jnp.bfloat16)
+    return table.reshape(cols, cols)
 
 
 def back_transform(filtered, table_part):

time: 199 us -> 131 us (0.66)
  other arithmetic: 105 us -> 37.8 us
    another operation x1, other arithmetic: 79.5 us -> 9.56 us
  transfers between devices with their start and end apart: 6 -> 6, of which waited for: 4 -> 3; matrix products, arithmetic and copies ran while one was open for 41% -> 10% of each run, Pallas kernels for 0% -> 0%
where the time goes in v1:
time: 131 us; the launch traced here: 130 us
  other arithmetic  37.8 us (29%)
  local copies, waits for them, and re-layouts  34.6 us (26%)
  starting transfers between devices  22.8 us (17%)
  matrix products  17.8 us (14%)
  waiting for transfers between devices  16.6 us (13%)
    scatter-add x1, other arithmetic, local(): surface = surface.at[:, dst_idx].add(incoming)  17.6 us
    dot_general x1, matrix products, back_transform(): lax.dot_general(filtered, table_part, (((1,), (1,)), ((), ())), preferred...  9.63 us
    another operation x1, other arithmetic  9.56 us
    gather x2, local copies, waits for them, and re-layouts, local(): outgoing = jnp.transpose(surface[:, src_idx] * weights[None], (1, 0, 2))  9.47 us
    all_to_all x1, waiting for transfers between devices, local(): incr = lax.all_to_all(incr, 'gy', split_axis=2, concat_axis=0, tiled=True)  8.62 us
    dot_general x1, matrix products, circle_increment(): jnp.dot(circles.reshape(-1, cols_all), table, preferred_element_type=jnp....  8.22 us
    all_to_all x1, starting transfers between devices, local(): lax.all_to_all(crossed, ('gx', 'gy'), split_axis=0, concat_axis=0, tiled=...  7.87 us
    all_to_all x1, waiting for transfers between devices, local(): lax.all_to_all(crossed, ('gx', 'gy'), split_axis=0, concat_axis=0, tiled=...  7.34 us
  transfers between devices with their start and end apart: 6, of which 3 were waited for; matrix products, arithmetic and copies ran while one was open for 10% of the time, Pallas kernels for 0%

profile of v1, /device:TPU:0, one launch (start us, length us, event | category | flops | bytes accessed | tf_op | source)
XLA Modules:
  0.0 129.7 jit_solution(9404093053873846128)
XLA Ops:
  0.0 0.0 copy-start
  0.0 0.0 copy-start.2
  0.0 0.0 copy-start.4
  0.0 1.1 fusion.37
  1.1 0.0 copy-start.1
  1.2 5.7 %copy.20 = f32[1,4,24,768]{1,3,2,0:T(8,128)} copy(f32[1,4,24,768]{3,2,1,0:T(8,128)S(1)} %get-tuple-element.7) | data formatting | bytes 589824 | tf_op jit(solution)/shard_map/slice | solution.py:92
  6.8 0.0 copy-done.2
  6.8 9.1 %gather_fusion = f32[2048,4]{1,0:T(8,128)S(1)} fusion(f32[4,18432]{0,1:T(8,128)} %bitcast.57, s32[2048]{0:T(1024)S(1)} %fusion.34), kind=kCustom, calls=%fused_computation | custom fusion | bytes 73728 | tf_op jit(solution)/shard_map/gather | solution.py:93
  16.0 0.3 copy.21
  16.3 0.0 copy-done.3
  16.3 0.0 copy-done.5
  16.3 0.1 bitcast_select_fusion
  16.4 0.6 collective-permute-start
  17.0 1.3 fusion.29
  18.3 1.6 %fusion.21 = (f32[64,1536]{1,0:T(8,128)S(1)}, f32[64,1536]{1,0:T(8,128)S(1)}) fusion(), kind=kLoop, calls=%fused_computation.30 | loop fusion | flops 884736 | bytes 786432 | tf_op jit(solution)/shard_map/sin | solution.py:37
  19.9 0.0 collective-permute-done
  19.9 0.6 copy.22
  20.5 7.9 %all-to-all-start = ((f32[16,4,128]{2,1,0:T(4,128)}), f32[16,4,128]{2,1,0:T(4,128)S(1)}, u32[]{:S(2)}, u32[]{:S(2)}) async-start(f32[16,4,128]{2,1,0:T(4,128)} %copy.22), calls=%async_computation | async-start | bytes 65536 | tf_op jit(solution)/shard_map/all_to_all | solution.py:95
  28.4 0.0 copy-done.4
  28.4 7.3 %all-to-all-done = f32[16,4,128]{2,1,0:T(4,128)S(1)} async-done(((f32[16,4,128]{2,1,0:T(4,128)}), f32[16,4,128]{2,1,0:T(4,128)S(1)}, u32[]{:S(2)}, u32[]{:S(2)}) %all-to-all-start) | async-done | bytes 32800 | tf_op jit(solution)/shard_map/all_to_all | solution.py:95
  35.7 0.4 copy.23
  36.1 17.6 %scatter_fusion = f32[4,18432]{0,1:T(8,128)} fusion(f32[4,18432]{0,1:T(8,128)} %bitcast.58, s32[2048]{0:T(1024)S(1)} %fusion.32, f32[2048,4]{1,0:T(8,128)S(1)} %copy.23), kind=kCustom, calls=%fused_computation.1 | custom fusion | flops 8192 | bytes 106496 | tf_op jit(solution)/shard_map/scatter-add | solution.py:97
  53.7 6.4 %copy.24 = f32[4,24,768]{2,1,0:T(8,128)S(1)} copy(f32[4,24,768]{0,2,1:T(8,128)} %bitcast.59) | data formatting | bytes 589824 | tf_op jit(solution)/shard_map/reshape | solution.py:98
  60.1 0.0 copy-done.1
  60.1 0.7 fusion.16
  60.9 3.6 %all-to-all-start.1 = ((bf16[8,24,768]{2,1,0:T(8,128)(2,1)}), bf16[8,24,768]{2,1,0:T(8,128)(2,1)S(1)}, u32[]{:S(2)}, u32[]{:S(2)}) async-start(bf16[8,24,768]{2,1,0:T(8,128)(2,1)} %fusion.16), calls=%async_computation.1 | async-start | bytes 589824 | tf_op jit(solution)/shard_map/all_to_all | solution.py:101
  64.5 9.6 %subtract_convert_fusion = (bf16[48,64,1536]{2,1,0:T(8,128)(2,1)}, bf16[48,64,1536]{2,1,0:T(8,128)(2,1)}) fusion(f32[64,1536]{1,0:T(8,128)S(1)} %get-tuple-element.13, f32[48,1536]{1,0:T(8,128)S(1)} %get-tuple-element.12, f32[64,1536]{1,0:T(8,128)S(1)} %get-tuple-element.14, f32[48,1536]{1,0:T(8,128)S(1)} %get-tuple-element.11), kind=kLoop, calls=%fused_computation.6 | loop fusion | flops 37748736 | bytes 20250624 | tf_op jit(solution)/shard_map/convert.6
  74.1 0.0 copy-done
  74.1 0.0 all-to-all-done.1
  74.1 0.2 copy.29
  74.3 0.2 dot_general.8
  74.5 8.2 %fusion.7 = bf16[2,24,3072]{2,1,0:T(8,128)(2,1)S(1)} fusion(bf16[2,24,3072]{2,1,0:T(8,128)(2,1)S(1)} %dot_general.8, bf16[3072,1536]{1,0:T(8,128)(2,1)} %bitcast.62, bf16[3072,1536]{1,0:T(8,128)(2,1)} %bitcast.60, f32[2,3072]{1,0:T(2,128)S(1)} %dynamic-slice_bitcast_fusion), kind=kOutput, calls=%fused_computation.10 | convolution fusion | flops 944013312 | bytes 19488768 | tf_op jit(solution)/shard_map/dot_general | solution.py:57
  82.7 9.6 %fusion.10 = bf16[48,3072]{1,0:T(8,128)(2,1)S(1)} fusion(bf16[48,3072]{1,0:T(8,128)(2,1)S(1)} %bitcast.73, bf16[3072,1536]{1,0:T(8,128)(2,1)} %bitcast.63, bf16[3072,1536]{1,0:T(8,128)(2,1)} %bitcast.61), kind=kOutput, calls=%fused_computation.11 | convolution fusion | flops 944013312 | bytes 19464192 | tf_op jit(solution)/shard_map/dot_general | solution.py:50
  92.3 1.9 %copy.26 = bf16[2,24,3072]{1,0,2:T(2,128)(2,1)S(1)} copy(bf16[2,24,3072]{2,1,0:T(8,128)(2,1)S(1)} %bitcast.69) | data formatting | bytes 589824 | tf_op jit(solution)/shard_map/reshape | solution.py:61
  94.2 2.6 %reshape.245 = bf16[4,2,18432]{2,1,0:T(2,128)(2,1)} reshape(bf16[3072,2,24]{2,1,0:T(2,128)(2,1)S(1)} %bitcast.64) | data formatting | bytes 589824
  96.9 4.8 %all-to-all-start.2 = ((bf16[4,2,18432]{2,1,0:T(2,128)(2,1)}), bf16[4,2,18432]{2,1,0:T(2,128)(2,1)S(1)}, u32[]{:S(2)}, u32[]{:S(2)}) async-start(bf16[4,2,18432]{2,1,0:T(2,128)(2,1)} %reshape.245), calls=%async_computation.2 | async-start | bytes 589824 | tf_op jit(solution)/shard_map/all_to_all | solution.py:103
  101.7 8.6 %all-to-all-done.2 = bf16[4,2,18432]{2,1,0:T(2,128)(2,1)S(1)} async-done(((bf16[4,2,18432]{2,1,0:T(2,128)(2,1)}), bf16[4,2,18432]{2,1,0:T(2,128)(2,1)S(1)}, u32[]{:S(2)}, u32[]{:S(2)}) %all-to-all-start.2) | async-done | bytes 294944 | tf_op jit(solution)/shard_map/all_to_all | solution.py:103
  110.3 3.1 %reshape.246 = bf16[3072,2,24]{2,1,0:T(2,128)(2,1)} reshape(bf16[4,2,18432]{2,1,0:T(2,128)(2,1)S(1)} %all-to-all-done.2) | data formatting | bytes 589824
  113.5 2.5 %convert_bitcast_fusion = f32[4,2,24,768]{2,1,3,0:T(2,128)S(1)} fusion(bf16[2,24,4,768]{1,0,3,2:T(2,128)(2,1)} %bitcast.65), kind=kLoop, calls=%fused_computation.12 | loop fusion | flops 147456 | bytes 884736 | tf_op jit(solution)/shard_map/convert_element_type | solution.py:104
  115.9 2.9 %copy.27 = f32[4,2,24,768]{3,2,1,0:T(8,128)} copy(f32[4,2,24,768]{2,1,3,0:T(2,128)S(1)} %convert_bitcast_fusion) | data formatting | bytes 1179648 | tf_op jit(solution)/shard_map/convert_element_type | solution.py:104
  118.8 1.2 fusion.31
  120.1 1.3 collective-permute-start.2
  121.4 4.5 %collective-permute-start.1 = (bf16[8,1,768]{2,1,0:T(2,128)(2,1)S(1)}, bf16[8,1,768]{2,1,0:T(2,128)(2,1)S(1)}, u32[]{:S(2)}, u32[]{:S(2)}) collective-permute-start(bf16[8,1,768]{2,1,0:T(2,128)(2,1)S(1)} %get-tuple-element.9), channel_id=1, source_target_pairs={{0,4},{4,8},{8,12},{1,5},{5,9},{9,13},{2,6},{6,10},{10,14},{3,7},{... | collective-permute-start | bytes 36872 | tf_op jit(solution)/shard_map/ppermute | solution.py:16
  125.9 0.9 convert_select_fusion
  126.8 0.0 collective-permute-done.2
  126.8 0.6 collective-permute-done.1
  127.4 0.1 maximum_convert_fusion
  127.6 2.2 %fusion.15 = f32[1,8,24,768]{3,2,1,0:T(8,128)} fusion(f32[8,26,768]{2,1,0:T(8,128)S(1)} %maximum_convert_fusion, f32[24,768]{1,0:T(8,128)S(1)} %convert_select_fusion, f32[24,768]{1,0:T(8,128)} %bitcast.71, f32[4,2,24,768]{3,2,1,0:T(8,128)} %copy.27, f32[4,24,768]{2,1,0:T(8,128)} %copy-done.1, f32[4,24,768]{2,1,0:T(8,128)S(1)} %copy.24), kind=kLoop, calls=%fused_computation.19 | loop fusion | flops 1179648 | bytes 3096576 | tf_op jit(solution)/shard_map/broadcast_in_dim | solution.py:106
  (8 shorter events, 0.1 us)
Async XLA Ops:
  0.0 74.1 %copy-start = (f32[1,8,3072]{2,1,0:T(8,128)S(1)}, f32[1,8,3072]{2,1,0:T(8,128)}, u32[]{:S(2)}) copy-start(f32[1,8,3072]{2,1,0:T(8,128)} %param.9) | copy-start | bytes 294916
  0.0 6.8 %copy-start.2 = (s32[1,1,1,16,128]{4,3,2,1,0:T(8,128)S(1)}, s32[1,1,1,16,128]{4,3,2,1,0:T(8,128)}, u32[]{:S(2)}) copy-start(s32[1,1,1,16,128]{4,3,2,1,0:T(8,128)} %param.12) | copy-start | bytes 24580
  0.0 16.3 %copy-start.3 = (f32[1,1,1,16,128]{4,3,2,1,0:T(8,128)S(1)}, f32[1,1,1,16,128]{4,3,2,1,0:T(8,128)}, u32[]{:S(2)}) copy-start(f32[1,1,1,16,128]{4,3,2,1,0:T(8,128)} %param.14) | copy-start | bytes 24580
  0.0 16.3 %copy-start.5 = (s32[1,1,1,16]{3,2,1,0:T(1,128)S(1)}, s32[1,1,1,16]{3,2,1,0:T(1,128)}, u32[]{:S(2)}) copy-start(s32[1,1,1,16]{3,2,1,0:T(1,128)} %param.15) | copy-start | bytes 196
  0.0 28.4 %copy-start.4 = (s32[1,1,1,16,128]{4,3,2,1,0:T(8,128)S(1)}, s32[1,1,1,16,128]{4,3,2,1,0:T(8,128)}, u32[]{:S(2)}) copy-start(s32[1,1,1,16,128]{4,3,2,1,0:T(8,128)} %param.13) | copy-start | bytes 24580
  1.1 59.0 %copy-start.1 = (f32[4,24,768]{2,1,0:T(8,128)}, f32[4,24,768]{2,1,0:T(8,128)S(1)}, u32[]{:S(2)}) copy-start(f32[4,24,768]{2,1,0:T(8,128)S(1)} %get-tuple-element.8) | copy-start | bytes 884740
  16.4 3.5 %collective-permute-start = (f32[16,4,128]{2,0,1:T(8,128)S(1)}, f32[16,4,128]{2,0,1:T(8,128)S(1)}, u32[]{:S(2)}, u32[]{:S(2)}) collective-permute-start(f32[16,4,128]{2,0,1:T(8,128)S(1)} %multiply_bitcast_fusion), channel_id=1, source_target_pairs={{0,16},{16,0},{1,17},{17,1},{2,18},{18,2},{3,19},{19,3},{4,20},{20... | collective-permute-start | bytes 98312 | tf_op jit(solution)/shard_map/ppermute | solution.py:27
  20.5 15.2 %all-to-all-start = ((f32[16,4,128]{2,1,0:T(4,128)}), f32[16,4,128]{2,1,0:T(4,128)S(1)}, u32[]{:S(2)}, u32[]{:S(2)}) async-start(f32[16,4,128]{2,1,0:T(4,128)} %copy.22), calls=%async_computation | async-start | bytes 65536 | tf_op jit(solution)/shard_map/all_to_all | solution.py:95
  60.9 13.2 %all-to-all-start.1 = ((bf16[8,24,768]{2,1,0:T(8,128)(2,1)}), bf16[8,24,768]{2,1,0:T(8,128)(2,1)S(1)}, u32[]{:S(2)}, u32[]{:S(2)}) async-start(bf16[8,24,768]{2,1,0:T(8,128)(2,1)} %fusion.16), calls=%async_computation.1 | async-start | bytes 589824 | tf_op jit(solution)/shard_map/all_to_all | solution.py:101
  96.9 13.5 %all-to-all-start.2 = ((bf16[4,2,18432]{2,1,0:T(2,128)(2,1)}), bf16[4,2,18432]{2,1,0:T(2,128)(2,1)S(1)}, u32[]{:S(2)}, u32[]{:S(2)}) async-start(bf16[4,2,18432]{2,1,0:T(2,128)(2,1)} %reshape.245), calls=%async_computation.2 | async-start | bytes 589824 | tf_op jit(solution)/shard_map/all_to_all | solution.py:103
  120.1 6.8 %collective-permute-start.2 = (bf16[8,1,768]{2,1,0:T(2,128)(2,1)S(1)}, bf16[8,1,768]{2,1,0:T(2,128)(2,1)S(1)}, u32[]{:S(2)}, u32[]{:S(2)}) collective-permute-start(bf16[8,1,768]{2,1,0:T(2,128)(2,1)S(1)} %get-tuple-element.10), channel_id=1, source_target_pairs={{4,0},{8,4},{12,8},{5,1},{9,5},{13,9},{6,2},{10,6},{14,10},{7,3},{... | collective-permute-start | bytes 36872 | tf_op jit(solution)/shard_map/ppermute | solution.py:19
  121.4 6.1 %collective-permute-start.1 = (bf16[8,1,768]{2,1,0:T(2,128)(2,1)S(1)}, bf16[8,1,768]{2,1,0:T(2,128)(2,1)S(1)}, u32[]{:S(2)}, u32[]{:S(2)}) collective-permute-start(bf16[8,1,768]{2,1,0:T(2,128)(2,1)S(1)} %get-tuple-element.9), channel_id=1, source_target_pairs={{0,4},{4,8},{8,12},{1,5},{5,9},{9,13},{2,6},{6,10},{10,14},{3,7},{... | collective-permute-start | bytes 36872 | tf_op jit(solution)/shard_map/ppermute | solution.py:16

commit v2 on v1

--- a/solution.py
+++ b/solution.py
@@ -66,6 +66,39 @@
     return fields + rate[None] * (padded[:, 2:] + padded[:, :-2] - 2.0 * fields)
 
 
+def split3(values):
+    high = values.astype(jnp.bfloat16)
+    rest = values - high.astype(jnp.float32)
+    mid = rest.astype(jnp.bfloat16)
+    low = (rest - mid.astype(jnp.float32)).astype(jnp.bfloat16)
+    return jnp.concatenate([high, mid, low], axis=0)
+
+
+def exact_dot(values, onehot):
+    rows = values.shape[0]
+    out = jnp.dot(split3(values), onehot, preferred_element_type=jnp.float32)
+    return out[:rows] + out[rows : 2 * rows] + out[2 * rows :]
+
+
+def gather_cells(surface, index):
+    fc, rows_dev, cols_dev = surface.shape
+    row, col = index // cols_dev, index % cols_dev
+    onehot = (jnp.arange(cols_dev, dtype=jnp.int32)[:, None] == col[None, :]).astype(jnp.bfloat16)
+    picked = exact_dot(surface.reshape(fc * rows_dev, cols_dev), onehot)
+    picked = picked.reshape(fc, rows_dev, -1)
+    mask = jnp.arange(rows_dev, dtype=jnp.int32)[:, None] == row[None, :]
+    return jnp.sum(jnp.where(mask[None], picked, 0.0), axis=1)
+
+
+def scatter_cells(values, index, rows_dev, cols_dev):
+    fc = values.shape[0]
+    row, col = index // cols_dev, index % cols_dev
+    mask = jnp.arange(rows_dev, dtype=jnp.int32)[:, None] == row[None, :]
+    spread = jnp.where(mask[None], values[:, None, :], 0.0).reshape(fc * rows_dev, -1)
+    onehot = (col[:, None] == jnp.arange(cols_dev, dtype=jnp.int32)[None, :]).astype(jnp.bfloat16)
+    return exact_dot(spread, onehot).reshape(fc, rows_dev, cols_dev)
+
+
 def local(
     state, response, diffusion, land_mask, couple_src, couple_dst, couple_weight, couple_count
 ):
@@ -89,13 +122,13 @@
     resp_mine = lax.dynamic_slice_in_dim(response[0], first_level, per_level, 0)
     rate = diffusion[0]
     fields = state[0]
-    surface = fields[:FC].reshape(FC, cells)
-    outgoing = jnp.transpose(surface[:, src_idx] * weights[None], (1, 0, 2))
+    surface = fields[:FC]
+    picked = gather_cells(surface, src_idx.reshape(-1)).reshape(FC, peers, slots)
+    outgoing = jnp.transpose(picked * weights[None], (1, 0, 2))
     crossed = partner(outgoing, "comp", 0)
     arrived = lax.all_to_all(crossed, ("gx", "gy"), split_axis=0, concat_axis=0, tiled=True)
-    incoming = jnp.transpose(arrived, (1, 0, 2))
-    surface = surface.at[:, dst_idx].add(incoming)
-    surf = surface.reshape(FC, rows_dev, cols_dev)
+    incoming = jnp.transpose(arrived, (1, 0, 2)).reshape(FC, peers * slots)
+    surf = surface + scatter_cells(incoming, dst_idx.reshape(-1), rows_dev, cols_dev)
     fields = jnp.concatenate([surf, fields[FC:]], axis=0)
     grid_bf = fields.astype(jnp.bfloat16)
     circles = lax.all_to_all(grid_bf, "gy", split_axis=0, concat_axis=2, tiled=True)

time: 131 us -> 93.1 us (0.71)
  local copies, waits for them, and re-layouts: 34.6 us -> 12.1 us
  other arithmetic: 37.8 us -> 21.6 us
  matrix products: 17.8 us -> 20.6 us
  waiting for transfers between devices: 16.6 us -> 15 us
    scatter-add x1 -> x0, other arithmetic: 17.6 us -> none  [local(): surface = surface.at[:, dst_idx].add(incoming)]
    gather x2 -> x0, local copies, waits for them, and re-layouts: 9.47 us -> none  [local(): outgoing = jnp.transpose(surface[:, src_idx] * weights[None], (1, 0, 2))]
    reshape x1 -> x0, local copies, waits for them, and re-layouts: 6.37 us -> none  [local(): surf = surface.reshape(FC, rows_dev, cols_dev)]
    slice x2 -> x1, local copies, waits for them, and re-layouts: 6.78 us -> 1.12 us  [local(): surface = fields[:FC]]
    dot_general x0 -> x2, matrix products: none -> 2.72 us  [exact_dot(): out = jnp.dot(split3(values), onehot, preferred_element_type=jnp.float32)]
    all_to_all x1, waiting for transfers between devices: 7.34 us -> 5.76 us  [local(): lax.all_to_all(crossed, ('gx', 'gy'), split_axis=0, concat_axis=0, tiled=...]
  transfers between devices with their start and end apart: 6 -> 6, of which waited for: 3 -> 3; matrix products, arithmetic and copies ran while one was open for 10% -> 15% of each run, Pallas kernels for 0% -> 0%
where the time goes in v2:
time: 93.1 us; the launch traced here: 92.2 us
  starting transfers between devices  22.8 us (24%)
  other arithmetic  21.6 us (23%)
  matrix products  20.6 us (22%)
  waiting for transfers between devices  15 us (16%)
  local copies, waits for them, and re-layouts  12.1 us (13%)
    dot_general x1, matrix products, back_transform(): lax.dot_general(filtered, table_part, (((1,), (1,)), ((), ())), preferred...  9.63 us
    another operation x1, other arithmetic  9.58 us
    all_to_all x1, waiting for transfers between devices, local(): incr = lax.all_to_all(incr, 'gy', split_axis=2, concat_axis=0, tiled=True)  8.62 us
    dot_general x1, matrix products, circle_increment(): jnp.dot(circles.reshape(-1, cols_all), table, preferred_element_type=jnp....  8.22 us
    all_to_all x1, starting transfers between devices, local(): lax.all_to_all(crossed, ('gx', 'gy'), split_axis=0, concat_axis=0, tiled=...  7.9 us
    unnamed x14, local copies, waits for them, and re-layouts  5.78 us
    all_to_all x1, waiting for transfers between devices, local(): lax.all_to_all(crossed, ('gx', 'gy'), split_axis=0, concat_axis=0, tiled=...  5.76 us
    all_to_all x1, starting transfers between devices, local(): incr = lax.all_to_all(incr, 'gy', split_axis=2, concat_axis=0, tiled=True)  4.85 us
  transfers between devices with their start and end apart: 6, of which 3 were waited for; matrix products, arithmetic and copies ran while one was open for 15% of the time, Pallas kernels for 0%

profile of v2, /device:TPU:0, one launch (start us, length us, event | category | flops | bytes accessed | tf_op | source)
XLA Modules:
  0.0 92.2 jit_solution(11216852830713089252)
XLA Ops:
  0.0 0.0 copy-start
  0.0 0.0 copy-start.4
  0.0 1.1 %fusion.59 = (f32[1,4,24,768]{3,2,1,0:T(8,128)S(1)}, f32[4,24,768]{2,1,0:T(8,128)S(1)}) fusion(f32[1,8,24,768]{3,2,1,0:T(8,128)} %param.8), kind=kLoop, calls=%fused_computation.102 | loop fusion | bytes 1179648 | tf_op jit(solution)/shard_map/slice | solution.py:125
  1.1 0.0 copy-start.1
  1.2 0.7 add_select_fusion.4
  2.0 1.2 %fusion.3 = f32[288,2048]{1,0:T(8,128)S(1)} fusion(s32[2048]{0:T(1024)S(1)} %get-tuple-element.18, bf16[96,768]{1,0:T(8,128)(2,1)S(1)} %get-tuple-element.14, bf16[96,768]{1,0:T(8,128)(2,1)S(1)} %get-tuple-element.13, bf16[96,768]{1,0:T(8,128)(2,1)S(1)} %bitcast_convert_fusion.1), kind=kOutput, calls=%fused_computation.8 | convolution fusion | flops 908869632 | bytes 2809856 | tf_op jit(solution)/shard_map/dot_general | solution.py:79
  3.2 0.0 copy-start.2
  3.2 0.1 slice_add_fusion
  3.4 0.1 select_reduce_fusion
  3.5 0.0 copy-done.4
  3.5 0.0 copy-done.5
  3.5 0.1 bitcast_select_fusion
  3.6 0.6 collective-permute-start
  4.2 0.0 copy-done.3
  4.2 1.3 %fusion.44 = (f32[48,1536]{1,0:T(8,128)S(1)}, f32[48,1536]{1,0:T(8,128)S(1)}) fusion(s32[48]{0:T(128)S(1)} %iota_multiply_fusion), kind=kLoop, calls=%fused_computation.67 | loop fusion | flops 663552 | bytes 590016 | tf_op jit(solution)/shard_map/cos | solution.py:37
  5.5 0.0 collective-permute-done
  5.5 7.9 %all-to-all-start = ((f32[16,4,128]{2,1,0:T(4,128)}), f32[16,4,128]{2,1,0:T(4,128)S(1)}, u32[]{:S(2)}, u32[]{:S(2)}) async-start(f32[16,4,128]{2,1,0:T(4,128)} %collective-permute-done), calls=%async_computation | async-start | bytes 65536 | tf_op jit(solution)/shard_map/all_to_all | solution.py:129
  13.4 1.6 %fusion.36 = (f32[64,1536]{1,0:T(8,128)S(1)}, f32[64,1536]{1,0:T(8,128)S(1)}) fusion(), kind=kLoop, calls=%fused_computation.51 | loop fusion | flops 884736 | bytes 786432 | tf_op jit(solution)/shard_map/sin | solution.py:37
  15.0 5.8 %all-to-all-done = f32[16,4,128]{2,1,0:T(4,128)S(1)} async-done(((f32[16,4,128]{2,1,0:T(4,128)}), f32[16,4,128]{2,1,0:T(4,128)S(1)}, u32[]{:S(2)}, u32[]{:S(2)}) %all-to-all-start) | async-done | bytes 32800 | tf_op jit(solution)/shard_map/all_to_all | solution.py:129
  20.8 0.1 broadcast_select_fusion
  20.9 0.1 fusion.25
  21.0 1.5 %fusion.4 = f32[288,768]{1,0:T(8,128)S(1)} fusion(s32[2048]{0:T(1024)S(1)} %get-tuple-element.16, bf16[96,2048]{1,0:T(8,128)(2,1)S(1)} %get-tuple-element.8, bf16[96,2048]{1,0:T(8,128)(2,1)S(1)} %get-tuple-element.7, bf16[96,2048]{1,0:T(8,128)(2,1)S(1)} %bitcast_convert_fusion), kind=kOutput, calls=%fused_computation.9 | convolution fusion | flops 911081472 | bytes 2072576 | tf_op jit(solution)/shard_map/dot_general | solution.py:79
  22.6 0.0 copy-done.2
  22.6 0.0 copy-done.1
  22.6 0.7 fusion.26
  23.4 3.6 %all-to-all-start.1 = ((bf16[8,24,768]{2,1,0:T(8,128)(2,1)}), bf16[8,24,768]{2,1,0:T(8,128)(2,1)S(1)}, u32[]{:S(2)}, u32[]{:S(2)}) async-start(bf16[8,24,768]{2,1,0:T(8,128)(2,1)} %fusion.26), calls=%async_computation.1 | async-start | bytes 589824 | tf_op jit(solution)/shard_map/all_to_all | solution.py:134
  27.0 9.6 %subtract_convert_fusion = (bf16[48,64,1536]{2,1,0:T(8,128)(2,1)}, bf16[48,64,1536]{2,1,0:T(8,128)(2,1)}) fusion(f32[64,1536]{1,0:T(8,128)S(1)} %get-tuple-element.21, f32[48,1536]{1,0:T(8,128)S(1)} %get-tuple-element.20, f32[64,1536]{1,0:T(8,128)S(1)} %get-tuple-element.22, f32[48,1536]{1,0:T(8,128)S(1)} %get-tuple-element.19), kind=kLoop, calls=%fused_computation.4 | loop fusion | flops 37748736 | bytes 20250624 | tf_op jit(solution)/shard_map/convert.6
  36.6 0.0 copy-done
  36.6 0.0 all-to-all-done.1
  36.6 0.2 copy.15
  36.8 0.2 dot_general.16
  37.0 8.2 %fusion.9 = bf16[2,24,3072]{2,1,0:T(8,128)(2,1)S(1)} fusion(bf16[2,24,3072]{2,1,0:T(8,128)(2,1)S(1)} %dot_general.16, bf16[3072,1536]{1,0:T(8,128)(2,1)} %bitcast.120, bf16[3072,1536]{1,0:T(8,128)(2,1)} %bitcast.118, f32[2,3072]{1,0:T(2,128)S(1)} %dynamic-slice_bitcast_fusion), kind=kOutput, calls=%fused_computation.12 | convolution fusion | flops 944013312 | bytes 19488768 | tf_op jit(solution)/shard_map/dot_general | solution.py:57
  45.2 9.6 %fusion.12 = bf16[48,3072]{1,0:T(8,128)(2,1)S(1)} fusion(bf16[48,3072]{1,0:T(8,128)(2,1)S(1)} %bitcast.132, bf16[3072,1536]{1,0:T(8,128)(2,1)} %bitcast.121, bf16[3072,1536]{1,0:T(8,128)(2,1)} %bitcast.119), kind=kOutput, calls=%fused_computation.13 | convolution fusion | flops 944013312 | bytes 19464192 | tf_op jit(solution)/shard_map/dot_general | solution.py:50
  54.9 1.9 %copy.12 = bf16[2,24,3072]{1,0,2:T(2,128)(2,1)S(1)} copy(bf16[2,24,3072]{2,1,0:T(8,128)(2,1)S(1)} %bitcast.128) | data formatting | bytes 589824 | tf_op jit(solution)/shard_map/reshape | solution.py:61
  56.8 2.6 %reshape.284 = bf16[4,2,18432]{2,1,0:T(2,128)(2,1)} reshape(bf16[3072,2,24]{2,1,0:T(2,128)(2,1)S(1)} %bitcast.122) | data formatting | bytes 589824
  59.4 4.8 %all-to-all-start.2 = ((bf16[4,2,18432]{2,1,0:T(2,128)(2,1)}), bf16[4,2,18432]{2,1,0:T(2,128)(2,1)S(1)}, u32[]{:S(2)}, u32[]{:S(2)}) async-start(bf16[4,2,18432]{2,1,0:T(2,128)(2,1)} %reshape.284), calls=%async_computation.2 | async-start | bytes 589824 | tf_op jit(solution)/shard_map/all_to_all | solution.py:136
  64.3 8.6 %all-to-all-done.2 = bf16[4,2,18432]{2,1,0:T(2,128)(2,1)S(1)} async-done(((bf16[4,2,18432]{2,1,0:T(2,128)(2,1)}), bf16[4,2,18432]{2,1,0:T(2,128)(2,1)S(1)}, u32[]{:S(2)}, u32[]{:S(2)}) %all-to-all-start.2) | async-done | bytes 294944 | tf_op jit(solution)/shard_map/all_to_all | solution.py:136
  72.9 3.1 %reshape.285 = bf16[3072,2,24]{2,1,0:T(2,128)(2,1)} reshape(bf16[4,2,18432]{2,1,0:T(2,128)(2,1)S(1)} %all-to-all-done.2) | data formatting | bytes 589824
  76.0 2.5 %convert_bitcast_fusion = f32[4,2,24,768]{2,1,3,0:T(2,128)S(1)} fusion(bf16[2,24,4,768]{1,0,3,2:T(2,128)(2,1)} %bitcast.123), kind=kLoop, calls=%fused_computation.14 | loop fusion | flops 147456 | bytes 884736 | tf_op jit(solution)/shard_map/convert_element_type | solution.py:137
  78.5 2.8 %copy.13 = f32[4,2,24,768]{3,2,1,0:T(8,128)} copy(f32[4,2,24,768]{2,1,3,0:T(2,128)S(1)} %convert_bitcast_fusion) | data formatting | bytes 1179648 | tf_op jit(solution)/shard_map/convert_element_type | solution.py:137
  81.3 1.2 %fusion.47 = bf16[8,24,768]{2,1,0:T(8,128)(2,1)S(1)} fusion(f32[4,2,24,768]{3,2,1,0:T(8,128)} %copy.13, f32[4,24,768]{2,1,0:T(8,128)} %copy-done.1, f32[4,24,768]{2,1,0:T(8,128)S(1)} %bitcast_add_fusion.1), kind=kLoop, calls=%fused_computation.74 | loop fusion | flops 442368 | bytes 1474560 | tf_op jit(solution)/shard_map/convert_element_type | solution.py:65
  82.6 1.3 %collective-permute-start.2 = (bf16[8,1,768]{2,1,0:T(2,128)(2,1)S(1)}, bf16[8,1,768]{2,1,0:T(2,128)(2,1)S(1)}, u32[]{:S(2)}, u32[]{:S(2)}) collective-permute-start(bf16[8,1,768]{2,1,0:T(2,128)(2,1)S(1)} %get-tuple-element.12), channel_id=1, source_target_pairs={{4,0},{8,4},{12,8},{5,1},{9,5},{13,9},{6,2},{10,6},{14,10},{7,3},{... | collective-permute-start | bytes 36872 | tf_op jit(solution)/shard_map/ppermute | solution.py:19
  83.9 4.5 %collective-permute-start.1 = (bf16[8,1,768]{2,1,0:T(2,128)(2,1)S(1)}, bf16[8,1,768]{2,1,0:T(2,128)(2,1)S(1)}, u32[]{:S(2)}, u32[]{:S(2)}) collective-permute-start(bf16[8,1,768]{2,1,0:T(2,128)(2,1)S(1)} %get-tuple-element.11), channel_id=1, source_target_pairs={{0,4},{4,8},{8,12},{1,5},{5,9},{9,13},{2,6},{6,10},{10,14},{3,7},{... | collective-permute-start | bytes 36872 | tf_op jit(solution)/shard_map/ppermute | solution.py:16
  88.4 0.9 convert_select_fusion
  89.3 0.0 collective-permute-done.2
  89.3 0.6 collective-permute-done.1
  89.9 0.1 maximum_convert_fusion
  90.1 2.2 %fusion.24 = f32[1,8,24,768]{3,2,1,0:T(8,128)} fusion(f32[8,26,768]{2,1,0:T(8,128)S(1)} %maximum_convert_fusion, f32[24,768]{1,0:T(8,128)S(1)} %convert_select_fusion, f32[24,768]{1,0:T(8,128)} %bitcast.130, f32[4,2,24,768]{3,2,1,0:T(8,128)} %copy.13, f32[4,24,768]{2,1,0:T(8,128)} %copy-done.1, f32[4,24,768]{2,1,0:T(8,128)S(1)} %bitcast_add_fusion.1), kind=kLoop, calls=%fused_computation.34 | loop fusion | flops 1179648 | bytes 3096576 | tf_op jit(solution)/shard_map/broadcast_in_dim | solution.py:139
  (14 shorter events, 0.3 us)
Async XLA Ops:
  0.0 36.6 %copy-start = (f32[1,8,3072]{2,1,0:T(8,128)S(1)}, f32[1,8,3072]{2,1,0:T(8,128)}, u32[]{:S(2)}) copy-start(f32[1,8,3072]{2,1,0:T(8,128)} %param.9) | copy-start | bytes 294916
  0.0 3.5 %copy-start.4 = (f32[1,1,1,16,128]{4,3,2,1,0:T(8,128)S(1)}, f32[1,1,1,16,128]{4,3,2,1,0:T(8,128)}, u32[]{:S(2)}) copy-start(f32[1,1,1,16,128]{4,3,2,1,0:T(8,128)} %param.14) | copy-start | bytes 24580
  0.0 3.5 %copy-start.5 = (s32[1,1,1,16]{3,2,1,0:T(1,128)S(1)}, s32[1,1,1,16]{3,2,1,0:T(1,128)}, u32[]{:S(2)}) copy-start(s32[1,1,1,16]{3,2,1,0:T(1,128)} %param.15) | copy-start | bytes 196
  0.0 4.2 %copy-start.3 = (s32[1,1,1,16,128]{4,3,2,1,0:T(8,128)S(1)}, s32[1,1,1,16,128]{4,3,2,1,0:T(8,128)}, u32[]{:S(2)}) copy-start(s32[1,1,1,16,128]{4,3,2,1,0:T(8,128)} %param.13) | copy-start | bytes 24580
  1.1 21.5 %copy-start.1 = (f32[4,24,768]{2,1,0:T(8,128)}, f32[4,24,768]{2,1,0:T(8,128)S(1)}, u32[]{:S(2)}) copy-start(f32[4,24,768]{2,1,0:T(8,128)S(1)} %get-tuple-element.10) | copy-start | bytes 884740
  3.2 19.4 %copy-start.2 = (f32[1,8,24,768]{3,2,1,0:T(8,128)S(1)}, f32[1,8,24,768]{3,2,1,0:T(8,128)}, u32[]{:S(2)}) copy-start(f32[1,8,24,768]{3,2,1,0:T(8,128)} %param.8) | copy-start | bytes 1769476
  3.6 1.9 %collective-permute-start = (f32[16,4,128]{2,1,0:T(4,128)S(1)}, f32[16,4,128]{2,1,0:T(4,128)}, u32[]{:S(2)}, u32[]{:S(2)}) collective-permute-start(f32[16,4,128]{2,1,0:T(4,128)S(1)} %fusion.48), channel_id=1, source_target_pairs={{0,16},{16,0},{1,17},{17,1},{2,18},{18,2},{3,19},{19,3},{4,20},{20... | collective-permute-start | bytes 98312 | tf_op jit(solution)/shard_map/ppermute | solution.py:27
  5.5 15.3 %all-to-all-start = ((f32[16,4,128]{2,1,0:T(4,128)}), f32[16,4,128]{2,1,0:T(4,128)S(1)}, u32[]{:S(2)}, u32[]{:S(2)}) async-start(f32[16,4,128]{2,1,0:T(4,128)} %collective-permute-done), calls=%async_computation | async-start | bytes 65536 | tf_op jit(solution)/shard_map/all_to_all | solution.py:129
  23.4 13.2 %all-to-all-start.1 = ((bf16[8,24,768]{2,1,0:T(8,128)(2,1)}), bf16[8,24,768]{2,1,0:T(8,128)(2,1)S(1)}, u32[]{:S(2)}, u32[]{:S(2)}) async-start(bf16[8,24,768]{2,1,0:T(8,128)(2,1)} %fusion.26), calls=%async_computation.1 | async-start | bytes 589824 | tf_op jit(solution)/shard_map/all_to_all | solution.py:134
  59.4 13.5 %all-to-all-start.2 = ((bf16[4,2,18432]{2,1,0:T(2,128)(2,1)}), bf16[4,2,18432]{2,1,0:T(2,128)(2,1)S(1)}, u32[]{:S(2)}, u32[]{:S(2)}) async-start(bf16[4,2,18432]{2,1,0:T(2,128)(2,1)} %reshape.284), calls=%async_computation.2 | async-start | bytes 589824 | tf_op jit(solution)/shard_map/all_to_all | solution.py:136
  82.6 6.8 %collective-permute-start.2 = (bf16[8,1,768]{2,1,0:T(2,128)(2,1)S(1)}, bf16[8,1,768]{2,1,0:T(2,128)(2,1)S(1)}, u32[]{:S(2)}, u32[]{:S(2)}) collective-permute-start(bf16[8,1,768]{2,1,0:T(2,128)(2,1)S(1)} %get-tuple-element.12), channel_id=1, source_target_pairs={{4,0},{8,4},{12,8},{5,1},{9,5},{13,9},{6,2},{10,6},{14,10},{7,3},{... | collective-permute-start | bytes 36872 | tf_op jit(solution)/shard_map/ppermute | solution.py:19
  83.9 6.1 %collective-permute-start.1 = (bf16[8,1,768]{2,1,0:T(2,128)(2,1)S(1)}, bf16[8,1,768]{2,1,0:T(2,128)(2,1)S(1)}, u32[]{:S(2)}, u32[]{:S(2)}) collective-permute-start(bf16[8,1,768]{2,1,0:T(2,128)(2,1)S(1)} %get-tuple-element.11), channel_id=1, source_target_pairs={{0,4},{4,8},{8,12},{1,5},{5,9},{9,13},{2,6},{6,10},{10,14},{3,7},{... | collective-permute-start | bytes 36872 | tf_op jit(solution)/shard_map/ppermute | solution.py:16

commit v3 on v2

--- a/solution.py
+++ b/solution.py
@@ -27,8 +27,8 @@
     return lax.ppermute(value, axis, pairs)
 
 
-def make_table(cols):
-    split = 64 if cols % 64 == 0 else 1
+def make_table(cols, rows):
+    split = 64 if rows % 64 == 0 else 1
     wave_idx = jnp.arange(cols // 2, dtype=jnp.int32)[None, :]
     scale = 2.0 * math.pi / cols
 
@@ -36,14 +36,14 @@
         angle = (rows_idx * wave_idx % cols).astype(jnp.float32) * scale
         return jnp.cos(angle), jnp.sin(angle)
 
-    cos_hi, sin_hi = trig(jnp.arange(cols // split, dtype=jnp.int32)[:, None] * split)
+    cos_hi, sin_hi = trig(jnp.arange(rows // split, dtype=jnp.int32)[:, None] * split)
     cos_lo, sin_lo = trig(jnp.arange(split, dtype=jnp.int32)[:, None])
     cos_hi, sin_hi = cos_hi[:, None], sin_hi[:, None]
     cos_lo, sin_lo = cos_lo[None], sin_lo[None]
     cos_all = cos_hi * cos_lo - sin_hi * sin_lo
     sin_all = sin_hi * cos_lo + cos_hi * sin_lo
     table = jnp.concatenate([cos_all, sin_all], axis=2).astype(jnp.bfloat16)
-    return table.reshape(cols, cols)
+    return table.reshape(rows, cols)
 
 
 def back_transform(filtered, table_part):
@@ -54,10 +54,22 @@
 
 def circle_increment(circles, resp_part, table, scale):
     count, rows_part, cols_all = circles.shape
-    spec = jnp.dot(circles.reshape(-1, cols_all), table, preferred_element_type=jnp.float32)
+    half = cols_all // 2
+    grid = circles.reshape(-1, cols_all)
+    lines = grid.shape[0]
+    sign = jnp.where(jnp.arange(cols_all, dtype=jnp.int32) % 2 == 0, 1.0, -1.0)
+    both = jnp.dot(
+        jnp.concatenate([grid[:, :half], grid[:, half:]], axis=0),
+        table,
+        preferred_element_type=jnp.float32,
+    )
+    spec = both[:lines] + sign[None, :] * both[lines:]
     spec = spec.reshape(count, rows_part, cols_all)
-    filtered = (spec * resp_part[:, None, :]).astype(jnp.bfloat16)
-    incr = (back_transform(filtered.reshape(-1, cols_all), table) * scale).astype(jnp.bfloat16)
+    filtered = (spec * resp_part[:, None, :]).astype(jnp.bfloat16).reshape(lines, cols_all)
+    flipped = filtered * sign.astype(jnp.bfloat16)[None, :]
+    back = back_transform(jnp.concatenate([filtered, flipped], axis=0), table)
+    incr = jnp.concatenate([back[:lines], back[lines:]], axis=1)
+    incr = (incr * scale).astype(jnp.bfloat16)
     return incr.reshape(count, rows_part, cols_all)
 
 
@@ -112,7 +124,7 @@
     per_level = levels // groups_y
     section = lax.axis_index("comp")
     keep = jnp.where(section == 1, land_mask.astype(jnp.float32), jnp.float32(1.0))
-    table = make_table(cols_all)
+    table = make_table(cols_all, cols_all // 2)
     scale = 2.0 / cols_all
     src_idx = couple_src.reshape(peers, slots)
     dst_idx = couple_dst.reshape(peers, slots)

time: 93.1 us -> 88.8 us (0.954)
  waiting for transfers between devices: 15 us -> 27.8 us
  matrix products: 20.6 us -> 10.8 us
  other arithmetic: 21.6 us -> 16.8 us
  starting transfers between devices: 22.8 us -> 19.4 us
  local copies, waits for them, and re-layouts: 12.1 us -> 13.1 us
    all_to_all x1, waiting for transfers between devices: 0.01 us -> 9.04 us  [local(): lax.all_to_all(grid_bf, 'gy', split_axis=0, concat_axis=2, tiled=True)]
    dot_general x1, matrix products: 9.63 us -> 2.94 us  [back_transform(): lax.dot_general(filtered, table_part, (((1,), (1,)), ((), ())), preferred...]
    another operation x1, other arithmetic: 9.58 us -> 5.21 us
    ppermute x1, waiting for transfers between devices: 0.01 us -> 3.52 us  [extended(): lax.ppermute(lax.slice_in_dim(block, 0, width, axis=dim), axis, backward)]
    dot_general x1, matrix products: 8.22 us -> 5.11 us  [circle_increment(): jnp.dot(jnp.concatenate([grid[:, :half], grid[:, half:]], axis=0), table,...]
    ppermute x1, starting transfers between devices: 4.55 us -> 2.56 us  [extended(): lax.ppermute(lax.slice_in_dim(block, block.shape[dim] - width, None, axis...]
    reshape x1 -> x0, local copies, waits for them, and re-layouts: 1.89 us -> none  [circle_increment(): return incr.reshape(count, rows_part, cols_all)]
    convert_element_type x0 -> x1, local copies, waits for them, and re-layouts: none -> 1.89 us  [circle_increment(): incr = (incr * scale).astype(jnp.bfloat16)]
  transfers between devices with their start and end apart: 6 -> 6, of which waited for: 3 -> 4; matrix products, arithmetic and copies ran while one was open for 15% -> 10% of each run, Pallas kernels for 0% -> 0%
where the time goes in v3:
time: 88.8 us; the launch traced here: 88.2 us
  waiting for transfers between devices  27.8 us (31%)
  starting transfers between devices  19.4 us (22%)
  other arithmetic  16.8 us (19%)
  local copies, waits for them, and re-layouts  13.1 us (15%)
  matrix products  10.8 us (12%)
    all_to_all x1, waiting for transfers between devices, local(): lax.all_to_all(grid_bf, 'gy', split_axis=0, concat_axis=2, tiled=True)  9.04 us
    all_to_all x1, waiting for transfers between devices, local(): incr = lax.all_to_all(incr, 'gy', split_axis=2, concat_axis=0, tiled=True)  7.95 us
    all_to_all x1, starting transfers between devices, local(): lax.all_to_all(crossed, ('gx', 'gy'), split_axis=0, concat_axis=0, tiled=...  7.88 us
    all_to_all x1, waiting for transfers between devices, local(): lax.all_to_all(crossed, ('gx', 'gy'), split_axis=0, concat_axis=0, tiled=...  7.31 us
    unnamed x23, local copies, waits for them, and re-layouts  6.93 us
    another operation x1, other arithmetic  5.21 us
    dot_general x1, matrix products, circle_increment(): jnp.dot(jnp.concatenate([grid[:, :half], grid[:, half:]], axis=0), table,...  5.11 us
    all_to_all x1, starting transfers between devices, local(): incr = lax.all_to_all(incr, 'gy', split_axis=2, concat_axis=0, tiled=True)  3.63 us
  transfers between devices with their start and end apart: 6, of which 4 were waited for; matrix products, arithmetic and copies ran while one was open for 10% of the time, Pallas kernels for 0%

profile of v3, /device:TPU:0, one launch (start us, length us, event | category | flops | bytes accessed | tf_op | source)
XLA Modules:
  0.0 88.2 jit_solution(7377589431821764047)
XLA Ops:
  0.0 1.1 %fusion.68 = (f32[1,4,24,768]{3,2,1,0:T(8,128)S(1)}, f32[4,24,768]{2,1,0:T(8,128)S(1)}) fusion(f32[1,8,24,768]{3,2,1,0:T(8,128)} %param.8), kind=kLoop, calls=%fused_computation.118 | loop fusion | bytes 1179648 | tf_op jit(solution)/shard_map/slice | solution.py:137
  1.2 0.7 add_select_fusion.5
  2.0 0.0 copy-start.4
  2.0 0.0 copy-start.5
  2.0 1.2 %fusion = f32[288,2048]{1,0:T(8,128)S(1)} fusion(s32[2048]{0:T(1024)S(1)} %get-tuple-element.24, bf16[96,768]{1,0:T(8,128)(2,1)S(1)} %get-tuple-element.20, bf16[96,768]{1,0:T(8,128)(2,1)S(1)} %get-tuple-element.19, bf16[96,768]{1,0:T(8,128)(2,1)S(1)} %bitcast_convert_fusion.1), kind=kOutput, calls=%fused_computation.5 | convolution fusion | flops 908869632 | bytes 2809856 | tf_op jit(solution)/shard_map/dot_general | solution.py:91
  3.2 0.1 slice_add_fusion
  3.4 0.1 select_reduce_fusion
  3.6 0.1 bitcast_select_fusion
  3.6 0.6 collective-permute-start
  4.2 1.6 %fusion.34 = (f32[64,1536]{1,0:T(8,128)S(1)}, f32[64,1536]{1,0:T(8,128)S(1)}) fusion(), kind=kLoop, calls=%fused_computation.54 | loop fusion | flops 884736 | bytes 786432 | tf_op jit(solution)/shard_map/sin | solution.py:37
  5.8 0.7 fusion.47
  6.5 0.0 copy-start.3
  6.5 5.2 %subtract_convert_fusion = (bf16[24,64,1536]{2,1,0:T(8,128)(2,1)}, bf16[24,64,1536]{2,1,0:T(8,128)(2,1)}) fusion(f32[64,1536]{1,0:T(8,128)S(1)} %get-tuple-element.27, f32[24,1536]{1,0:T(8,128)S(1)} %get-tuple-element.26, f32[64,1536]{1,0:T(8,128)S(1)} %get-tuple-element.28, f32[24,1536]{1,0:T(8,128)S(1)} %get-tuple-element.25), kind=kLoop, calls=%fused_computation.2 | loop fusion | flops 18874368 | bytes 10518528 | tf_op jit(solution)/shard_map/convert.6
  11.7 0.0 collective-permute-done
  11.7 7.9 %all-to-all-start = ((f32[16,4,128]{2,1,0:T(4,128)}), f32[16,4,128]{2,1,0:T(4,128)S(1)}, u32[]{:S(2)}, u32[]{:S(2)}) async-start(f32[16,4,128]{2,1,0:T(4,128)} %collective-permute-done), calls=%async_computation | async-start | bytes 65536 | tf_op jit(solution)/shard_map/all_to_all | solution.py:141
  19.7 7.3 %all-to-all-done = f32[16,4,128]{2,1,0:T(4,128)S(1)} async-done(((f32[16,4,128]{2,1,0:T(4,128)}), f32[16,4,128]{2,1,0:T(4,128)S(1)}, u32[]{:S(2)}, u32[]{:S(2)}) %all-to-all-start) | async-done | bytes 32800 | tf_op jit(solution)/shard_map/all_to_all | solution.py:141
  27.0 0.1 broadcast_select_fusion
  27.0 0.1 fusion.23
  27.2 0.0 copy-start.2
  27.2 1.5 %fusion.1 = f32[288,768]{1,0:T(8,128)S(1)} fusion(s32[2048]{0:T(1024)S(1)} %get-tuple-element.22, bf16[96,2048]{1,0:T(8,128)(2,1)S(1)} %get-tuple-element.10, bf16[96,2048]{1,0:T(8,128)(2,1)S(1)} %get-tuple-element.9, bf16[96,2048]{1,0:T(8,128)(2,1)S(1)} %bitcast_convert_fusion), kind=kOutput, calls=%fused_computation.6 | convolution fusion | flops 911081472 | bytes 2072576 | tf_op jit(solution)/shard_map/dot_general | solution.py:91
  28.8 0.7 fusion.24
  29.6 3.5 %all-to-all-start.1 = ((bf16[8,24,768]{2,1,0:T(8,128)(2,1)}), bf16[8,24,768]{2,1,0:T(8,128)(2,1)S(1)}, u32[]{:S(2)}, u32[]{:S(2)}) async-start(bf16[8,24,768]{2,1,0:T(8,128)(2,1)} %fusion.24), calls=%async_computation.1 | async-start | bytes 589824 | tf_op jit(solution)/shard_map/all_to_all | solution.py:146
  33.1 9.0 %all-to-all-done.1 = bf16[8,24,768]{2,1,0:T(8,128)(2,1)S(1)} async-done(((bf16[8,24,768]{2,1,0:T(8,128)(2,1)}), bf16[8,24,768]{2,1,0:T(8,128)(2,1)S(1)}, u32[]{:S(2)}, u32[]{:S(2)}) %all-to-all-start.1) | async-done | bytes 294944 | tf_op jit(solution)/shard_map/all_to_all | solution.py:146
  42.1 0.2 copy.20
  42.3 0.0 slice-start
  42.3 0.0 slice-start.2
  42.4 0.0 slice-start.1
  42.4 0.0 slice-start.3
  42.4 5.1 %fusion.3 = f32[96,3072]{1,0:T(8,128)S(1)} fusion(bf16[1536,1536]{1,0:T(8,128)(2,1)} %bitcast.119, bf16[1536,1536]{1,0:T(8,128)(2,1)} %bitcast.115, bf16[48,1536]{1,0:T(8,128)(2,1)S(1)} %get-tuple-element.18, bf16[48,1536]{1,0:T(8,128)(2,1)S(1)} %get-tuple-element.17), kind=kOutput, calls=%fused_computation.8 | convolution fusion | flops 925433856 | bytes 10911744 | tf_op jit(solution)/shard_map/dot_general | solution.py:61
  47.5 0.1 broadcast_multiply_fusion
  47.6 0.9 %slice-done.2 = s8[4194304]{0:T(1024)(128)(4,1)S(1)} async-done(((s8[4718592]{0:T(1024)(128)(4,1)}), s8[4194304]{0:T(1024)(128)(4,1)S(1)}, s32[]{:S(2)}) %slice-start.2) | async-done | bytes 4194328
  48.5 0.0 slice-done.1
  48.6 0.2 slice-done.3
  48.7 2.9 %fusion.2 = f32[96,1536]{1,0:T(8,128)S(1)} fusion(bf16[1536,1536]{1,0:T(8,128)(2,1)S(1)} %bitcast.122, bf16[1536,1536]{1,0:T(8,128)(2,1)S(1)} %bitcast.118, bf16[48,3072]{1,0:T(8,128)(2,1)S(1)} %get-tuple-element.5, bf16[48,3072]{1,0:T(8,128)(2,1)S(1)} %get-tuple-element.6), kind=kOutput, calls=%fused_computation.7 | convolution fusion | flops 926023680 | bytes 10616832 | tf_op jit(solution)/shard_map/dot_general | solution.py:50
  51.8 1.9 %copy.21 = bf16[2,24,3072]{1,0,2:T(2,128)(2,1)S(1)} copy(bf16[2,24,3072]{2,1,0:T(8,128)(2,1)S(1)} %fusion.22) | data formatting | bytes 589824 | tf_op jit(solution)/shard_map/convert_element_type | solution.py:72
  53.7 2.6 %reshape.295 = bf16[4,2,18432]{2,1,0:T(2,128)(2,1)} reshape(bf16[3072,2,24]{2,1,0:T(2,128)(2,1)S(1)} %bitcast.113) | data formatting | bytes 589824
  56.3 3.6 %all-to-all-start.2 = ((bf16[4,2,18432]{2,1,0:T(2,128)(2,1)}), bf16[4,2,18432]{2,1,0:T(2,128)(2,1)S(1)}, u32[]{:S(2)}, u32[]{:S(2)}) async-start(bf16[4,2,18432]{2,1,0:T(2,128)(2,1)} %reshape.295), calls=%async_computation.2 | async-start | bytes 589824 | tf_op jit(solution)/shard_map/all_to_all | solution.py:148
  60.0 8.0 %all-to-all-done.2 = bf16[4,2,18432]{2,1,0:T(2,128)(2,1)S(1)} async-done(((bf16[4,2,18432]{2,1,0:T(2,128)(2,1)}), bf16[4,2,18432]{2,1,0:T(2,128)(2,1)S(1)}, u32[]{:S(2)}, u32[]{:S(2)}) %all-to-all-start.2) | async-done | bytes 294944 | tf_op jit(solution)/shard_map/all_to_all | solution.py:148
  67.9 3.1 %reshape.296 = bf16[3072,2,24]{2,1,0:T(2,128)(2,1)} reshape(bf16[4,2,18432]{2,1,0:T(2,128)(2,1)S(1)} %all-to-all-done.2) | data formatting | bytes 589824
  71.0 2.5 %convert_bitcast_fusion = f32[4,2,24,768]{2,1,3,0:T(2,128)S(1)} fusion(bf16[2,24,4,768]{1,0,3,2:T(2,128)(2,1)} %bitcast.114), kind=kLoop, calls=%fused_computation.9 | loop fusion | flops 147456 | bytes 884736 | tf_op jit(solution)/shard_map/convert_element_type | solution.py:149
  73.5 2.9 %copy.22 = f32[4,2,24,768]{3,2,1,0:T(8,128)} copy(f32[4,2,24,768]{2,1,3,0:T(2,128)S(1)} %convert_bitcast_fusion) | data formatting | bytes 1179648 | tf_op jit(solution)/shard_map/convert_element_type | solution.py:149
  76.4 1.2 %fusion.41 = bf16[8,24,768]{2,1,0:T(8,128)(2,1)S(1)} fusion(f32[4,2,24,768]{3,2,1,0:T(8,128)} %copy.22, f32[4,24,768]{2,1,0:T(8,128)} %copy-done.1, f32[4,24,768]{2,1,0:T(8,128)S(1)} %bitcast_add_fusion.1), kind=kLoop, calls=%fused_computation.72 | loop fusion | flops 442368 | bytes 1474560 | tf_op jit(solution)/shard_map/convert_element_type | solution.py:77
  77.6 2.6 %collective-permute-start.1 = (bf16[8,1,768]{2,1,0:T(2,128)(2,1)S(1)}, bf16[8,1,768]{2,1,0:T(2,128)(2,1)S(1)}, u32[]{:S(2)}, u32[]{:S(2)}) collective-permute-start(bf16[8,1,768]{2,1,0:T(2,128)(2,1)S(1)} %get-tuple-element.15), channel_id=1, source_target_pairs={{0,4},{4,8},{8,12},{1,5},{5,9},{9,13},{2,6},{6,10},{10,14},{3,7},{... | collective-permute-start | bytes 36872 | tf_op jit(solution)/shard_map/ppermute | solution.py:16
  80.2 1.3 %collective-permute-start.2 = (bf16[8,1,768]{2,1,0:T(2,128)(2,1)S(1)}, bf16[8,1,768]{2,1,0:T(2,128)(2,1)S(1)}, u32[]{:S(2)}, u32[]{:S(2)}) collective-permute-start(bf16[8,1,768]{2,1,0:T(2,128)(2,1)S(1)} %get-tuple-element.16), channel_id=1, source_target_pairs={{4,0},{8,4},{12,8},{5,1},{9,5},{13,9},{6,2},{10,6},{14,10},{7,3},{... | collective-permute-start | bytes 36872 | tf_op jit(solution)/shard_map/ppermute | solution.py:19
  81.5 0.9 %convert_select_fusion = f32[24,768]{1,0:T(8,128)S(1)} fusion(s32[24,768]{1,0:T(8,128)} %param.11, pred[]{:T(512)S(6)} %eq.98), kind=kLoop, calls=%fused_computation.82 | loop fusion | flops 36864 | bytes 147457 | tf_op jit(solution)/shard_map/jit(_where)/select_n | solution.py:126
  82.4 3.5 %collective-permute-done.2 = bf16[8,1,768]{2,1,0:T(2,128)(2,1)S(1)} collective-permute-done((bf16[8,1,768]{2,1,0:T(2,128)(2,1)S(1)}, bf16[8,1,768]{2,1,0:T(2,128)(2,1)S(1)}, u32[]{:S(2)}, u32[]{:S(2)}) %collective-permute-start.2) | collective-permute-done | bytes 12320 | tf_op jit(solution)/shard_map/ppermute | solution.py:19
  85.9 0.1 maximum_convert_fusion
  86.1 2.2 %fusion.15 = f32[1,8,24,768]{3,2,1,0:T(8,128)} fusion(f32[8,26,768]{2,1,0:T(8,128)S(1)} %maximum_convert_fusion, f32[24,768]{1,0:T(8,128)S(1)} %convert_select_fusion, f32[24,768]{1,0:T(8,128)} %bitcast.131, f32[4,2,24,768]{3,2,1,0:T(8,128)} %copy.22, f32[4,24,768]{2,1,0:T(8,128)} %copy-done.1, f32[4,24,768]{2,1,0:T(8,128)S(1)} %bitcast_add_fusion.1), kind=kLoop, calls=%fused_computation.29 | loop fusion | flops 1179648 | bytes 3096576 | tf_op jit(solution)/shard_map/broadcast_in_dim | solution.py:151
  (29 shorter events, 0.5 us)
Async XLA Ops:
  0.0 33.0 %copy-start = (f32[1,8,3072]{2,1,0:T(8,128)S(1)}, f32[1,8,3072]{2,1,0:T(8,128)}, u32[]{:S(2)}) copy-start(f32[1,8,3072]{2,1,0:T(8,128)} %param.9) | copy-start | bytes 294916
  1.1 27.7 %copy-start.1 = (f32[4,24,768]{2,1,0:T(8,128)}, f32[4,24,768]{2,1,0:T(8,128)S(1)}, u32[]{:S(2)}) copy-start(f32[4,24,768]{2,1,0:T(8,128)S(1)} %get-tuple-element.14) | copy-start | bytes 884740
  2.0 1.6 %copy-start.4 = (f32[1,1,1,16,128]{4,3,2,1,0:T(8,128)S(1)}, f32[1,1,1,16,128]{4,3,2,1,0:T(8,128)}, u32[]{:S(2)}) copy-start(f32[1,1,1,16,128]{4,3,2,1,0:T(8,128)} %param.14) | copy-start | bytes 24580
  2.0 1.6 %copy-start.5 = (s32[1,1,1,16]{3,2,1,0:T(1,128)S(1)}, s32[1,1,1,16]{3,2,1,0:T(1,128)}, u32[]{:S(2)}) copy-start(s32[1,1,1,16]{3,2,1,0:T(1,128)} %param.15) | copy-start | bytes 196
  3.6 8.1 %collective-permute-start = (f32[16,4,128]{2,1,0:T(4,128)S(1)}, f32[16,4,128]{2,1,0:T(4,128)}, u32[]{:S(2)}, u32[]{:S(2)}) collective-permute-start(f32[16,4,128]{2,1,0:T(4,128)S(1)} %fusion.49), channel_id=1, source_target_pairs={{0,16},{16,0},{1,17},{17,1},{2,18},{18,2},{3,19},{19,3},{4,20},{20... | collective-permute-start | bytes 98312 | tf_op jit(solution)/shard_map/ppermute | solution.py:27
  6.5 5.2 %copy-start.3 = (s32[1,1,1,16,128]{4,3,2,1,0:T(8,128)S(1)}, s32[1,1,1,16,128]{4,3,2,1,0:T(8,128)}, u32[]{:S(2)}) copy-start(s32[1,1,1,16,128]{4,3,2,1,0:T(8,128)} %param.13) | copy-start | bytes 24580
  11.7 15.2 %all-to-all-start = ((f32[16,4,128]{2,1,0:T(4,128)}), f32[16,4,128]{2,1,0:T(4,128)S(1)}, u32[]{:S(2)}, u32[]{:S(2)}) async-start(f32[16,4,128]{2,1,0:T(4,128)} %collective-permute-done), calls=%async_computation | async-start | bytes 65536 | tf_op jit(solution)/shard_map/all_to_all | solution.py:141
  27.2 1.6 %copy-start.2 = (f32[1,8,24,768]{3,2,1,0:T(8,128)S(1)}, f32[1,8,24,768]{3,2,1,0:T(8,128)}, u32[]{:S(2)}) copy-start(f32[1,8,24,768]{3,2,1,0:T(8,128)} %param.8) | copy-start | bytes 1769476
  29.6 12.5 %all-to-all-start.1 = ((bf16[8,24,768]{2,1,0:T(8,128)(2,1)}), bf16[8,24,768]{2,1,0:T(8,128)(2,1)S(1)}, u32[]{:S(2)}, u32[]{:S(2)}) async-start(bf16[8,24,768]{2,1,0:T(8,128)(2,1)} %fusion.24), calls=%async_computation.1 | async-start | bytes 589824 | tf_op jit(solution)/shard_map/all_to_all | solution.py:146
  42.3 5.3 %slice-start = ((s8[4718592]{0:T(1024)(128)(4,1)}), s8[4194304]{0:T(1024)(128)(4,1)S(1)}, s32[]{:S(2)}) async-start(s8[4718592]{0:T(1024)(128)(4,1)} %bitcast.116), calls=%async_computation.3 | async-start | bytes 8388608
  42.3 6.2 %slice-start.2 = ((s8[4718592]{0:T(1024)(128)(4,1)}), s8[4194304]{0:T(1024)(128)(4,1)S(1)}, s32[]{:S(2)}) async-start(s8[4718592]{0:T(1024)(128)(4,1)} %bitcast.120), calls=%async_computation.5 | async-start | bytes 8388608
  42.4 6.2 %slice-start.1 = ((s8[4718592]{0:T(1024)(128)(4,1)}), s8[524288]{0:T(1024)(128)(4,1)S(1)}, s32[]{:S(2)}) async-start(s8[4718592]{0:T(1024)(128)(4,1)} %bitcast.116), calls=%async_computation.4 | async-start | bytes 1048576
  42.4 6.4 %slice-start.3 = ((s8[4718592]{0:T(1024)(128)(4,1)}), s8[524288]{0:T(1024)(128)(4,1)S(1)}, s32[]{:S(2)}) async-start(s8[4718592]{0:T(1024)(128)(4,1)} %bitcast.120), calls=%async_computation.6 | async-start | bytes 1048576
  56.3 11.6 %all-to-all-start.2 = ((bf16[4,2,18432]{2,1,0:T(2,128)(2,1)}), bf16[4,2,18432]{2,1,0:T(2,128)(2,1)S(1)}, u32[]{:S(2)}, u32[]{:S(2)}) async-start(bf16[4,2,18432]{2,1,0:T(2,128)(2,1)} %reshape.295), calls=%async_computation.2 | async-start | bytes 589824 | tf_op jit(solution)/shard_map/all_to_all | solution.py:148
  77.6 4.8 %collective-permute-start.1 = (bf16[8,1,768]{2,1,0:T(2,128)(2,1)S(1)}, bf16[8,1,768]{2,1,0:T(2,128)(2,1)S(1)}, u32[]{:S(2)}, u32[]{:S(2)}) collective-permute-start(bf16[8,1,768]{2,1,0:T(2,128)(2,1)S(1)} %get-tuple-element.15), channel_id=1, source_target_pairs={{0,4},{4,8},{8,12},{1,5},{5,9},{9,13},{2,6},{6,10},{10,14},{3,7},{... | collective-permute-start | bytes 36872 | tf_op jit(solution)/shard_map/ppermute | solution.py:16
  80.2 5.7 %collective-permute-start.2 = (bf16[8,1,768]{2,1,0:T(2,128)(2,1)S(1)}, bf16[8,1,768]{2,1,0:T(2,128)(2,1)S(1)}, u32[]{:S(2)}, u32[]{:S(2)}) collective-permute-start(bf16[8,1,768]{2,1,0:T(2,128)(2,1)S(1)} %get-tuple-element.16), channel_id=1, source_target_pairs={{4,0},{8,4},{12,8},{5,1},{9,5},{13,9},{6,2},{10,6},{14,10},{7,3},{... | collective-permute-start | bytes 36872 | tf_op jit(solution)/shard_map/ppermute | solution.py:19

commit v4 on v3

--- a/solution.py
+++ b/solution.py
@@ -137,8 +137,12 @@
     surface = fields[:FC]
     picked = gather_cells(surface, src_idx.reshape(-1)).reshape(FC, peers, slots)
     outgoing = jnp.transpose(picked * weights[None], (1, 0, 2))
-    crossed = partner(outgoing, "comp", 0)
-    arrived = lax.all_to_all(crossed, ("gx", "gy"), split_axis=0, concat_axis=0, tiled=True)
+    other = (1 - section) * peers
+    spread = jnp.concatenate([outgoing, outgoing], axis=0)
+    target = jnp.arange(2 * peers, dtype=jnp.int32)[:, None, None] // peers == 1 - section
+    spread = jnp.where(target, spread, jnp.float32(0.0))
+    mixed = lax.all_to_all(spread, ("comp", "gx", "gy"), split_axis=0, concat_axis=0, tiled=True)
+    arrived = lax.dynamic_slice_in_dim(mixed, other, peers, 0)
     incoming = jnp.transpose(arrived, (1, 0, 2)).reshape(FC, peers * slots)
     surf = surface + scatter_cells(incoming, dst_idx.reshape(-1), rows_dev, cols_dev)
     fields = jnp.concatenate([surf, fields[FC:]], axis=0)

time: 88.8 us -> 84.2 us (0.948)
  waiting for transfers between devices: 27.8 us -> 21.3 us
  starting transfers between devices: 19.4 us -> 20.5 us
    all_to_all x1, waiting for transfers between devices: 7.31 us -> 0.01 us  [local(): lax.all_to_all(spread, ('comp', 'gx', 'gy'), split_axis=0, concat_axis=0,...]
    all_to_all x1, starting transfers between devices: 3.45 us -> 4.89 us  [local(): lax.all_to_all(grid_bf, 'gy', split_axis=0, concat_axis=2, tiled=True)]
  transfers between devices with their start and end apart: 6 -> 5, of which waited for: 4 -> 3; matrix products, arithmetic and copies ran while one was open for 10% -> 10% of each run, Pallas kernels for 0% -> 0%
where the time goes in v4:
time: 84.2 us; the launch traced here: 83.7 us
  waiting for transfers between devices  21.3 us (25%)
  starting transfers between devices  20.5 us (24%)
  other arithmetic  17.6 us (21%)
  local copies, waits for them, and re-layouts  13.1 us (16%)
  matrix products  10.8 us (13%)
    all_to_all x1, waiting for transfers between devices, local(): lax.all_to_all(grid_bf, 'gy', split_axis=0, concat_axis=2, tiled=True)  9.87 us
    all_to_all x1, waiting for transfers between devices, local(): incr = lax.all_to_all(incr, 'gy', split_axis=2, concat_axis=0, tiled=True)  7.95 us
    all_to_all x1, starting transfers between devices, local(): lax.all_to_all(spread, ('comp', 'gx', 'gy'), split_axis=0, concat_axis=0,...  7.32 us
    unnamed x23, local copies, waits for them, and re-layouts  6.93 us
    another operation x1, other arithmetic  5.25 us
    dot_general x1, matrix products, circle_increment(): jnp.dot(jnp.concatenate([grid[:, :half], grid[:, half:]], axis=0), table,...  5.11 us
    all_to_all x1, starting transfers between devices, local(): lax.all_to_all(grid_bf, 'gy', split_axis=0, concat_axis=2, tiled=True)  4.89 us
    all_to_all x1, starting transfers between devices, local(): incr = lax.all_to_all(incr, 'gy', split_axis=2, concat_axis=0, tiled=True)  3.63 us
  transfers between devices with their start and end apart: 5, of which 3 were waited for; matrix products, arithmetic and copies ran while one was open for 10% of the time, Pallas kernels for 0%

profile of v4, /device:TPU:0, one launch (start us, length us, event | category | flops | bytes accessed | tf_op | source)
XLA Modules:
  0.0 83.7 jit_solution(7865312193529387824)
XLA Ops:
  0.0 1.1 %fusion.69 = (f32[1,4,24,768]{3,2,1,0:T(8,128)S(1)}, f32[4,24,768]{2,1,0:T(8,128)S(1)}) fusion(f32[1,8,24,768]{3,2,1,0:T(8,128)} %param.8), kind=kLoop, calls=%fused_computation.125 | loop fusion | bytes 1179648 | tf_op jit(solution)/shard_map/slice | solution.py:137
  1.2 0.7 add_select_fusion.5
  2.0 0.0 copy-start.4
  2.0 0.0 copy-start.5
  2.0 0.0 copy-start.3
  2.0 1.2 %fusion = f32[288,2048]{1,0:T(8,128)S(1)} fusion(s32[2048]{0:T(1024)S(1)} %get-tuple-element.24, bf16[96,768]{1,0:T(8,128)(2,1)S(1)} %get-tuple-element.20, bf16[96,768]{1,0:T(8,128)(2,1)S(1)} %get-tuple-element.19, bf16[96,768]{1,0:T(8,128)(2,1)S(1)} %bitcast_convert_fusion.1), kind=kOutput, calls=%fused_computation.5 | convolution fusion | flops 908869632 | bytes 2809856 | tf_op jit(solution)/shard_map/dot_general | solution.py:91
  3.2 0.1 slice_add_fusion
  3.4 0.1 select_reduce_fusion
  3.6 0.1 bitcast_select_fusion
  3.7 0.7 maximum_select_fusion
  4.4 7.3 %all-to-all-start = ((f32[32,4,128]{2,1,0:T(4,128)}), f32[32,4,128]{2,1,0:T(4,128)S(1)}, u32[]{:S(2)}, u32[]{:S(2)}) async-start(f32[32,4,128]{2,1,0:T(4,128)} %maximum_select_fusion), calls=%async_computation | async-start | bytes 131072 | tf_op jit(solution)/shard_map/all_to_all | solution.py:144
  11.7 1.6 %fusion.34 = (f32[64,1536]{1,0:T(8,128)S(1)}, f32[64,1536]{1,0:T(8,128)S(1)}) fusion(), kind=kLoop, calls=%fused_computation.54 | loop fusion | flops 884736 | bytes 786432 | tf_op jit(solution)/shard_map/sin | solution.py:37
  13.4 0.7 fusion.47
  14.0 5.2 %subtract_convert_fusion = (bf16[24,64,1536]{2,1,0:T(8,128)(2,1)}, bf16[24,64,1536]{2,1,0:T(8,128)(2,1)}) fusion(f32[64,1536]{1,0:T(8,128)S(1)} %get-tuple-element.27, f32[24,1536]{1,0:T(8,128)S(1)} %get-tuple-element.26, f32[64,1536]{1,0:T(8,128)S(1)} %get-tuple-element.28, f32[24,1536]{1,0:T(8,128)S(1)} %get-tuple-element.25), kind=kLoop, calls=%fused_computation.2 | loop fusion | flops 18874368 | bytes 10518528 | tf_op jit(solution)/shard_map/convert.6
  19.3 0.0 all-to-all-done
  19.4 0.1 broadcast_select_fusion
  19.4 0.1 fusion.23
  19.6 0.0 copy-start.2
  19.6 1.5 %fusion.1 = f32[288,768]{1,0:T(8,128)S(1)} fusion(s32[2048]{0:T(1024)S(1)} %get-tuple-element.22, bf16[96,2048]{1,0:T(8,128)(2,1)S(1)} %get-tuple-element.10, bf16[96,2048]{1,0:T(8,128)(2,1)S(1)} %get-tuple-element.9, bf16[96,2048]{1,0:T(8,128)(2,1)S(1)} %bitcast_convert_fusion), kind=kOutput, calls=%fused_computation.6 | convolution fusion | flops 911081472 | bytes 2072576 | tf_op jit(solution)/shard_map/dot_general | solution.py:91
  21.2 0.7 fusion.24
  22.0 4.9 %all-to-all-start.1 = ((bf16[8,24,768]{2,1,0:T(8,128)(2,1)}), bf16[8,24,768]{2,1,0:T(8,128)(2,1)S(1)}, u32[]{:S(2)}, u32[]{:S(2)}) async-start(bf16[8,24,768]{2,1,0:T(8,128)(2,1)} %fusion.24), calls=%async_computation.1 | async-start | bytes 589824 | tf_op jit(solution)/shard_map/all_to_all | solution.py:150
  26.9 9.9 %all-to-all-done.1 = bf16[8,24,768]{2,1,0:T(8,128)(2,1)S(1)} async-done(((bf16[8,24,768]{2,1,0:T(8,128)(2,1)}), bf16[8,24,768]{2,1,0:T(8,128)(2,1)S(1)}, u32[]{:S(2)}, u32[]{:S(2)}) %all-to-all-start.1) | async-done | bytes 294944 | tf_op jit(solution)/shard_map/all_to_all | solution.py:150
  36.8 0.2 copy.20
  36.9 0.0 slice-start
  37.0 0.0 slice-start.2
  37.0 0.0 slice-start.1
  37.0 0.0 slice-start.3
  37.0 5.1 %fusion.3 = f32[96,3072]{1,0:T(8,128)S(1)} fusion(bf16[1536,1536]{1,0:T(8,128)(2,1)} %bitcast.120, bf16[1536,1536]{1,0:T(8,128)(2,1)} %bitcast.116, bf16[48,1536]{1,0:T(8,128)(2,1)S(1)} %get-tuple-element.18, bf16[48,1536]{1,0:T(8,128)(2,1)S(1)} %get-tuple-element.17), kind=kOutput, calls=%fused_computation.8 | convolution fusion | flops 925433856 | bytes 10911744 | tf_op jit(solution)/shard_map/dot_general | solution.py:61
  42.1 0.1 broadcast_multiply_fusion
  42.3 0.9 %slice-done.2 = s8[4194304]{0:T(1024)(128)(4,1)S(1)} async-done(((s8[4718592]{0:T(1024)(128)(4,1)}), s8[4194304]{0:T(1024)(128)(4,1)S(1)}, s32[]{:S(2)}) %slice-start.2) | async-done | bytes 4194328
  43.2 0.0 slice-done.1
  43.2 0.2 slice-done.3
  43.4 2.9 %fusion.2 = f32[96,1536]{1,0:T(8,128)S(1)} fusion(bf16[1536,1536]{1,0:T(8,128)(2,1)S(1)} %bitcast.123, bf16[1536,1536]{1,0:T(8,128)(2,1)S(1)} %bitcast.119, bf16[48,3072]{1,0:T(8,128)(2,1)S(1)} %get-tuple-element.5, bf16[48,3072]{1,0:T(8,128)(2,1)S(1)} %get-tuple-element.6), kind=kOutput, calls=%fused_computation.7 | convolution fusion | flops 926023680 | bytes 10616832 | tf_op jit(solution)/shard_map/dot_general | solution.py:50
  46.4 1.9 %copy.21 = bf16[2,24,3072]{1,0,2:T(2,128)(2,1)S(1)} copy(bf16[2,24,3072]{2,1,0:T(8,128)(2,1)S(1)} %fusion.22) | data formatting | bytes 589824 | tf_op jit(solution)/shard_map/convert_element_type | solution.py:72
  48.3 2.6 %reshape.334 = bf16[4,2,18432]{2,1,0:T(2,128)(2,1)} reshape(bf16[3072,2,24]{2,1,0:T(2,128)(2,1)S(1)} %bitcast.114) | data formatting | bytes 589824
  51.0 3.6 %all-to-all-start.2 = ((bf16[4,2,18432]{2,1,0:T(2,128)(2,1)}), bf16[4,2,18432]{2,1,0:T(2,128)(2,1)S(1)}, u32[]{:S(2)}, u32[]{:S(2)}) async-start(bf16[4,2,18432]{2,1,0:T(2,128)(2,1)} %reshape.334), calls=%async_computation.2 | async-start | bytes 589824 | tf_op jit(solution)/shard_map/all_to_all | solution.py:152
  54.6 8.0 %all-to-all-done.2 = bf16[4,2,18432]{2,1,0:T(2,128)(2,1)S(1)} async-done(((bf16[4,2,18432]{2,1,0:T(2,128)(2,1)}), bf16[4,2,18432]{2,1,0:T(2,128)(2,1)S(1)}, u32[]{:S(2)}, u32[]{:S(2)}) %all-to-all-start.2) | async-done | bytes 294944 | tf_op jit(solution)/shard_map/all_to_all | solution.py:152
  62.5 3.1 %reshape.335 = bf16[3072,2,24]{2,1,0:T(2,128)(2,1)} reshape(bf16[4,2,18432]{2,1,0:T(2,128)(2,1)S(1)} %all-to-all-done.2) | data formatting | bytes 589824
  65.7 2.5 %convert_bitcast_fusion = f32[4,2,24,768]{2,1,3,0:T(2,128)S(1)} fusion(bf16[2,24,4,768]{1,0,3,2:T(2,128)(2,1)} %bitcast.115), kind=kLoop, calls=%fused_computation.9 | loop fusion | flops 147456 | bytes 884736 | tf_op jit(solution)/shard_map/convert_element_type | solution.py:153
  68.2 2.8 %copy.22 = f32[4,2,24,768]{3,2,1,0:T(8,128)} copy(f32[4,2,24,768]{2,1,3,0:T(2,128)S(1)} %convert_bitcast_fusion) | data formatting | bytes 1179648 | tf_op jit(solution)/shard_map/convert_element_type | solution.py:153
  71.0 1.2 %fusion.41 = bf16[8,24,768]{2,1,0:T(8,128)(2,1)S(1)} fusion(f32[4,2,24,768]{3,2,1,0:T(8,128)} %copy.22, f32[4,24,768]{2,1,0:T(8,128)} %copy-done.1, f32[4,24,768]{2,1,0:T(8,128)S(1)} %bitcast_add_fusion.1), kind=kLoop, calls=%fused_computation.72 | loop fusion | flops 442368 | bytes 1474560 | tf_op jit(solution)/shard_map/convert_element_type | solution.py:77
  72.2 3.4 %collective-permute-start = (bf16[8,1,768]{2,1,0:T(2,128)(2,1)S(1)}, bf16[8,1,768]{2,1,0:T(2,128)(2,1)S(1)}, u32[]{:S(2)}, u32[]{:S(2)}) collective-permute-start(bf16[8,1,768]{2,1,0:T(2,128)(2,1)S(1)} %get-tuple-element.15), channel_id=1, source_target_pairs={{0,4},{4,8},{8,12},{1,5},{5,9},{9,13},{2,6},{6,10},{10,14},{3,7},{... | collective-permute-start | bytes 36872 | tf_op jit(solution)/shard_map/ppermute | solution.py:16
  75.6 1.3 %collective-permute-start.1 = (bf16[8,1,768]{2,1,0:T(2,128)(2,1)S(1)}, bf16[8,1,768]{2,1,0:T(2,128)(2,1)S(1)}, u32[]{:S(2)}, u32[]{:S(2)}) collective-permute-start(bf16[8,1,768]{2,1,0:T(2,128)(2,1)S(1)} %get-tuple-element.16), channel_id=1, source_target_pairs={{4,0},{8,4},{12,8},{5,1},{9,5},{13,9},{6,2},{10,6},{14,10},{7,3},{... | collective-permute-start | bytes 36872 | tf_op jit(solution)/shard_map/ppermute | solution.py:19
  76.9 0.9 %convert_select_fusion = f32[24,768]{1,0:T(8,128)S(1)} fusion(s32[24,768]{1,0:T(8,128)} %param.11, pred[]{:T(512)S(6)} %eq.111), kind=kLoop, calls=%fused_computation.82 | loop fusion | flops 36864 | bytes 147457 | tf_op jit(solution)/shard_map/jit(_where)/select_n | solution.py:126
  77.8 0.0 collective-permute-done
  77.8 3.5 %collective-permute-done.1 = bf16[8,1,768]{2,1,0:T(2,128)(2,1)S(1)} collective-permute-done((bf16[8,1,768]{2,1,0:T(2,128)(2,1)S(1)}, bf16[8,1,768]{2,1,0:T(2,128)(2,1)S(1)}, u32[]{:S(2)}, u32[]{:S(2)}) %collective-permute-start.1) | collective-permute-done | bytes 12320 | tf_op jit(solution)/shard_map/ppermute | solution.py:19
  81.4 0.1 maximum_convert_fusion
  81.5 2.2 %fusion.15 = f32[1,8,24,768]{3,2,1,0:T(8,128)} fusion(f32[8,26,768]{2,1,0:T(8,128)S(1)} %maximum_convert_fusion, f32[24,768]{1,0:T(8,128)S(1)} %convert_select_fusion, f32[24,768]{1,0:T(8,128)} %bitcast.131, f32[4,2,24,768]{3,2,1,0:T(8,128)} %copy.22, f32[4,24,768]{2,1,0:T(8,128)} %copy-done.1, f32[4,24,768]{2,1,0:T(8,128)S(1)} %bitcast_add_fusion.1), kind=kLoop, calls=%fused_computation.29 | loop fusion | flops 1179648 | bytes 3096576 | tf_op jit(solution)/shard_map/broadcast_in_dim | solution.py:155
  (30 shorter events, 0.5 us)
Async XLA Ops:
  0.0 26.9 %copy-start = (f32[1,8,3072]{2,1,0:T(8,128)S(1)}, f32[1,8,3072]{2,1,0:T(8,128)}, u32[]{:S(2)}) copy-start(f32[1,8,3072]{2,1,0:T(8,128)} %param.9) | copy-start | bytes 294916
  1.1 20.1 %copy-start.1 = (f32[4,24,768]{2,1,0:T(8,128)}, f32[4,24,768]{2,1,0:T(8,128)S(1)}, u32[]{:S(2)}) copy-start(f32[4,24,768]{2,1,0:T(8,128)S(1)} %get-tuple-element.14) | copy-start | bytes 884740
  2.0 1.6 %copy-start.4 = (f32[1,1,1,16,128]{4,3,2,1,0:T(8,128)S(1)}, f32[1,1,1,16,128]{4,3,2,1,0:T(8,128)}, u32[]{:S(2)}) copy-start(f32[1,1,1,16,128]{4,3,2,1,0:T(8,128)} %param.14) | copy-start | bytes 24580
  2.0 1.6 %copy-start.5 = (s32[1,1,1,16]{3,2,1,0:T(1,128)S(1)}, s32[1,1,1,16]{3,2,1,0:T(1,128)}, u32[]{:S(2)}) copy-start(s32[1,1,1,16]{3,2,1,0:T(1,128)} %param.15) | copy-start | bytes 196
  2.0 11.4 %copy-start.3 = (s32[1,1,1,16,128]{4,3,2,1,0:T(8,128)S(1)}, s32[1,1,1,16,128]{4,3,2,1,0:T(8,128)}, u32[]{:S(2)}) copy-start(s32[1,1,1,16,128]{4,3,2,1,0:T(8,128)} %param.13) | copy-start | bytes 24580
  4.4 14.9 %all-to-all-start = ((f32[32,4,128]{2,1,0:T(4,128)}), f32[32,4,128]{2,1,0:T(4,128)S(1)}, u32[]{:S(2)}, u32[]{:S(2)}) async-start(f32[32,4,128]{2,1,0:T(4,128)} %maximum_select_fusion), calls=%async_computation | async-start | bytes 131072 | tf_op jit(solution)/shard_map/all_to_all | solution.py:144
  19.6 1.6 %copy-start.2 = (f32[1,8,24,768]{3,2,1,0:T(8,128)S(1)}, f32[1,8,24,768]{3,2,1,0:T(8,128)}, u32[]{:S(2)}) copy-start(f32[1,8,24,768]{3,2,1,0:T(8,128)} %param.8) | copy-start | bytes 1769476
  22.0 14.8 %all-to-all-start.1 = ((bf16[8,24,768]{2,1,0:T(8,128)(2,1)}), bf16[8,24,768]{2,1,0:T(8,128)(2,1)S(1)}, u32[]{:S(2)}, u32[]{:S(2)}) async-start(bf16[8,24,768]{2,1,0:T(8,128)(2,1)} %fusion.24), calls=%async_computation.1 | async-start | bytes 589824 | tf_op jit(solution)/shard_map/all_to_all | solution.py:150
  36.9 5.3 %slice-start = ((s8[4718592]{0:T(1024)(128)(4,1)}), s8[4194304]{0:T(1024)(128)(4,1)S(1)}, s32[]{:S(2)}) async-start(s8[4718592]{0:T(1024)(128)(4,1)} %bitcast.117), calls=%async_computation.3 | async-start | bytes 8388608
  37.0 6.2 %slice-start.2 = ((s8[4718592]{0:T(1024)(128)(4,1)}), s8[4194304]{0:T(1024)(128)(4,1)S(1)}, s32[]{:S(2)}) async-start(s8[4718592]{0:T(1024)(128)(4,1)} %bitcast.121), calls=%async_computation.5 | async-start | bytes 8388608
  37.0 6.2 %slice-start.1 = ((s8[4718592]{0:T(1024)(128)(4,1)}), s8[524288]{0:T(1024)(128)(4,1)S(1)}, s32[]{:S(2)}) async-start(s8[4718592]{0:T(1024)(128)(4,1)} %bitcast.117), calls=%async_computation.4 | async-start | bytes 1048576
  37.0 6.4 %slice-start.3 = ((s8[4718592]{0:T(1024)(128)(4,1)}), s8[524288]{0:T(1024)(128)(4,1)S(1)}, s32[]{:S(2)}) async-start(s8[4718592]{0:T(1024)(128)(4,1)} %bitcast.121), calls=%async_computation.6 | async-start | bytes 1048576
  51.0 11.6 %all-to-all-start.2 = ((bf16[4,2,18432]{2,1,0:T(2,128)(2,1)}), bf16[4,2,18432]{2,1,0:T(2,128)(2,1)S(1)}, u32[]{:S(2)}, u32[]{:S(2)}) async-start(bf16[4,2,18432]{2,1,0:T(2,128)(2,1)} %reshape.334), calls=%async_computation.2 | async-start | bytes 589824 | tf_op jit(solution)/shard_map/all_to_all | solution.py:152
  72.2 5.6 %collective-permute-start = (bf16[8,1,768]{2,1,0:T(2,128)(2,1)S(1)}, bf16[8,1,768]{2,1,0:T(2,128)(2,1)S(1)}, u32[]{:S(2)}, u32[]{:S(2)}) collective-permute-start(bf16[8,1,768]{2,1,0:T(2,128)(2,1)S(1)} %get-tuple-element.15), channel_id=1, source_target_pairs={{0,4},{4,8},{8,12},{1,5},{5,9},{9,13},{2,6},{6,10},{10,14},{3,7},{... | collective-permute-start | bytes 36872 | tf_op jit(solution)/shard_map/ppermute | solution.py:16
  75.6 5.7 %collective-permute-start.1 = (bf16[8,1,768]{2,1,0:T(2,128)(2,1)S(1)}, bf16[8,1,768]{2,1,0:T(2,128)(2,1)S(1)}, u32[]{:S(2)}, u32[]{:S(2)}) collective-permute-start(bf16[8,1,768]{2,1,0:T(2,128)(2,1)S(1)} %get-tuple-element.16), channel_id=1, source_target_pairs={{4,0},{8,4},{12,8},{5,1},{9,5},{13,9},{6,2},{10,6},{14,10},{7,3},{... | collective-permute-start | bytes 36872 | tf_op jit(solution)/shard_map/ppermute | solution.py:19

commit v5 on v4

--- a/solution.py
+++ b/solution.py
@@ -52,25 +52,25 @@
     )
 
 
-def circle_increment(circles, resp_part, table, scale):
-    count, rows_part, cols_all = circles.shape
-    half = cols_all // 2
-    grid = circles.reshape(-1, cols_all)
-    lines = grid.shape[0]
+def circle_increment(blocks, resp_part, table, scale):
+    parts, count, rows_part, cols_dev = blocks.shape
+    cols_all = parts * cols_dev
+    lines = count * rows_part
     sign = jnp.where(jnp.arange(cols_all, dtype=jnp.int32) % 2 == 0, 1.0, -1.0)
-    both = jnp.dot(
-        jnp.concatenate([grid[:, :half], grid[:, half:]], axis=0),
-        table,
+    grid = blocks.reshape(2, parts // 2, lines, cols_dev)
+    both = lax.dot_general(
+        grid,
+        table.reshape(parts // 2, cols_dev, cols_all),
+        (((1, 3), (0, 1)), ((), ())),
         preferred_element_type=jnp.float32,
     )
-    spec = both[:lines] + sign[None, :] * both[lines:]
+    spec = both[0] + sign[None, :] * both[1]
     spec = spec.reshape(count, rows_part, cols_all)
     filtered = (spec * resp_part[:, None, :]).astype(jnp.bfloat16).reshape(lines, cols_all)
     flipped = filtered * sign.astype(jnp.bfloat16)[None, :]
     back = back_transform(jnp.concatenate([filtered, flipped], axis=0), table)
-    incr = jnp.concatenate([back[:lines], back[lines:]], axis=1)
-    incr = (incr * scale).astype(jnp.bfloat16)
-    return incr.reshape(count, rows_part, cols_all)
+    incr = (back * scale).astype(jnp.bfloat16).reshape(2, lines, parts // 2, cols_dev)
+    return jnp.transpose(incr, (0, 2, 1, 3)).reshape(parts, lines, cols_dev)
 
 
 def diffuse(fields, rate):
@@ -147,9 +147,11 @@
     surf = surface + scatter_cells(incoming, dst_idx.reshape(-1), rows_dev, cols_dev)
     fields = jnp.concatenate([surf, fields[FC:]], axis=0)
     grid_bf = fields.astype(jnp.bfloat16)
-    circles = lax.all_to_all(grid_bf, "gy", split_axis=0, concat_axis=2, tiled=True)
+    grid_bf = grid_bf.reshape(groups_y, per_level, rows_dev, cols_dev)
+    circles = lax.all_to_all(grid_bf, "gy", split_axis=0, concat_axis=0, tiled=True)
     incr = circle_increment(circles, resp_mine, table, scale)
-    incr = lax.all_to_all(incr, "gy", split_axis=2, concat_axis=0, tiled=True)
+    incr = lax.all_to_all(incr, "gy", split_axis=0, concat_axis=0, tiled=True)
+    incr = incr.reshape(levels, rows_dev, cols_dev)
     fields = fields + incr.astype(jnp.float32)
     fields = diffuse(fields, rate) * keep[None]
     return fields[None]

time: 84.2 us -> 70.2 us (0.83)
  local copies, waits for them, and re-layouts: 13.1 us -> 2.06 us
  other arithmetic: 17.6 us -> 11.8 us
  matrix products: 10.8 us -> 12.6 us
  waiting for transfers between devices: 21.3 us -> 22.4 us
    unnamed x23 -> x18, local copies, waits for them, and re-layouts: 6.93 us -> 0.05 us
    convert_element_type x2 -> x0, local copies, waits for them, and re-layouts: 4.72 us -> none  [the longest x1 2.84 us: local(): fields = fields + incr.astype(jnp.float32)]
    convert_element_type x2 -> x0, other arithmetic: 2.54 us -> none  [the longest x1 2.49 us: local(): fields = fields + incr.astype(jnp.float32)]
    dot_general x1, matrix products: 2.94 us -> 4.82 us  [back_transform(): lax.dot_general(filtered, table_part, (((1,), (1,)), ((), ())), preferred...]
    broadcast_in_dim x1, other arithmetic: 2.18 us -> 1.02 us  [local(): return fields[None]]
    convert_element_type x1, other arithmetic: 1.2 us -> 0.05 us  [diffuse(): fields.astype(jnp.bfloat16)]
    select_n x1, other arithmetic: 0.89 us -> 0.01 us  [local(): jnp.where(section == 1, land_mask.astype(jnp.float32), jnp.float32(1.0))]
  transfers between devices with their start and end apart: 5 -> 5, of which waited for: 3 -> 4; matrix products, arithmetic and copies ran while one was open for 10% -> 11% of each run, Pallas kernels for 0% -> 0%
where the time goes in v5:
time: 70.2 us; the launch traced here: 69.7 us
  waiting for transfers between devices  22.4 us (32%)
  starting transfers between devices  20.5 us (29%)
  matrix products  12.6 us (18%)
  other arithmetic  11.8 us (17%)
  local copies, waits for them, and re-layouts  2.06 us (3%)
    all_to_all x1, waiting for transfers between devices, local(): lax.all_to_all(grid_bf, 'gy', split_axis=0, concat_axis=0, tiled=True)  9.86 us
    all_to_all x1, waiting for transfers between devices, local(): incr = lax.all_to_all(incr, 'gy', split_axis=0, concat_axis=0, tiled=True)  8.13 us
    all_to_all x1, starting transfers between devices, local(): lax.all_to_all(spread, ('comp', 'gx', 'gy'), split_axis=0, concat_axis=0,...  7.33 us
    another operation x1, other arithmetic  5.22 us
    dot_general x1, matrix products, circle_increment(): lax.dot_general(grid, table.reshape(parts // 2, cols_dev, cols_all), (((1...  5.09 us
    all_to_all x1, starting transfers between devices, local(): lax.all_to_all(grid_bf, 'gy', split_axis=0, concat_axis=0, tiled=True)  5.02 us
    dot_general x1, matrix products, back_transform(): lax.dot_general(filtered, table_part, (((1,), (1,)), ((), ())), preferred...  4.82 us
    ppermute x1, waiting for transfers between devices, extended(): lax.ppermute(lax.slice_in_dim(block, 0, width, axis=dim), axis, backward)  4.22 us
  transfers between devices with their start and end apart: 5, of which 4 were waited for; matrix products, arithmetic and copies ran while one was open for 11% of the time, Pallas kernels for 0%

profile of v5, /device:TPU:0, one launch (start us, length us, event | category | flops | bytes accessed | tf_op | source)
XLA Modules:
  0.0 69.7 jit_solution(17490516444763896987)
XLA Ops:
  0.0 0.0 copy-start
  0.0 1.1 %fusion.75 = (f32[1,4,24,768]{3,2,1,0:T(8,128)S(1)}, f32[4,24,768]{2,1,0:T(8,128)S(1)}) fusion(f32[1,8,24,768]{3,2,1,0:T(8,128)} %param.8), kind=kLoop, calls=%fused_computation.126 | loop fusion | bytes 1179648 | tf_op jit(solution)/shard_map/slice | solution.py:137
  1.2 0.7 %add_select_fusion.5 = (s32[2048]{0:T(1024)S(1)}, s32[2048]{0:T(1024)S(1)}) fusion(s32[1,1,1,16,128]{4,3,2,1,0:T(8,128)} %param.12), kind=kLoop, calls=%fused_computation.97 | loop fusion | flops 24576 | bytes 24576 | tf_op jit(solution)/shard_map/jit(floor_divide)/jit(_where)/select_n | solution.py:97
  1.9 0.0 copy-start.5
  1.9 0.0 copy-start.6
  1.9 0.0 copy-start.4
  2.0 1.2 %fusion.5 = f32[288,2048]{1,0:T(8,128)S(1)} fusion(s32[2048]{0:T(1024)S(1)} %get-tuple-element.20, bf16[96,768]{1,0:T(8,128)(2,1)S(1)} %get-tuple-element.16, bf16[96,768]{1,0:T(8,128)(2,1)S(1)} %get-tuple-element.15, bf16[96,768]{1,0:T(8,128)(2,1)S(1)} %bitcast_convert_fusion.1), kind=kOutput, calls=%fused_computation.10 | convolution fusion | flops 908869632 | bytes 2809856 | tf_op jit(solution)/shard_map/dot_general | solution.py:91
  3.2 0.1 slice_add_fusion
  3.4 0.1 select_reduce_fusion
  3.5 0.0 copy-done.5
  3.5 0.0 copy-done.6
  3.5 0.1 bitcast_select_fusion
  3.6 0.7 %maximum_select_fusion = f32[32,4,128]{2,1,0:T(4,128)} fusion(f32[16,4,128]{2,1,0:T(4,128)S(1)} %fusion.56, pred[32]{0:T(512)(128)(4,1)S(1)} %fusion.69), kind=kLoop, calls=%fused_computation.85 | loop fusion | flops 32768 | bytes 98336 | tf_op jit(solution)/shard_map/jit(_where)/select_n | solution.py:143
  4.4 7.3 %all-to-all-start = ((f32[32,4,128]{2,1,0:T(4,128)}), f32[32,4,128]{2,1,0:T(4,128)S(1)}, u32[]{:S(2)}, u32[]{:S(2)}) async-start(f32[32,4,128]{2,1,0:T(4,128)} %maximum_select_fusion), calls=%async_computation | async-start | bytes 131072 | tf_op jit(solution)/shard_map/all_to_all | solution.py:144
  11.7 1.6 %fusion.44 = (f32[64,1536]{1,0:T(8,128)S(1)}, f32[64,1536]{1,0:T(8,128)S(1)}) fusion(), kind=kLoop, calls=%fused_computation.59 | loop fusion | flops 884736 | bytes 786432 | tf_op jit(solution)/shard_map/sin | solution.py:37
  13.3 0.0 copy-done.4
  13.3 0.7 fusion.54
  14.0 5.2 %subtract_convert_fusion = (bf16[24,64,1536]{2,1,0:T(8,128)(2,1)}, bf16[24,64,1536]{2,1,0:T(8,128)(2,1)}) fusion(f32[64,1536]{1,0:T(8,128)S(1)} %get-tuple-element.23, f32[24,1536]{1,0:T(8,128)S(1)} %get-tuple-element.22, f32[64,1536]{1,0:T(8,128)S(1)} %get-tuple-element.24, f32[24,1536]{1,0:T(8,128)S(1)} %get-tuple-element.21), kind=kLoop, calls=%fused_computation.6 | loop fusion | flops 18874368 | bytes 10518528 | tf_op jit(solution)/shard_map/convert.8
  19.3 0.0 all-to-all-done
  19.3 0.1 broadcast_select_fusion
  19.4 0.1 fusion.33
  19.5 0.0 copy-start.1
  19.5 1.5 %fusion.6 = f32[288,768]{1,0:T(8,128)S(1)} fusion(s32[2048]{0:T(1024)S(1)} %get-tuple-element.18, bf16[96,2048]{1,0:T(8,128)(2,1)S(1)} %get-tuple-element.10, bf16[96,2048]{1,0:T(8,128)(2,1)S(1)} %get-tuple-element.9, bf16[96,2048]{1,0:T(8,128)(2,1)S(1)} %bitcast_convert_fusion), kind=kOutput, calls=%fused_computation.11 | convolution fusion | flops 911081472 | bytes 2072576 | tf_op jit(solution)/shard_map/dot_general | solution.py:91
  21.1 0.0 copy-done.1
  21.1 0.7 %fusion.34 = bf16[8,24,768]{2,1,0:T(8,128)(2,1)} fusion(f32[4,24,768]{2,1,0:T(8,128)S(1)} %get-tuple-element.12, f32[4,24,768]{2,1,0:T(8,128)S(1)} %bitcast_add_fusion), kind=kLoop, calls=%fused_computation.47 | loop fusion | flops 147456 | bytes 884736 | tf_op jit(solution)/shard_map/convert_element_type | solution.py:149
  21.9 5.0 %all-to-all-start.1 = ((bf16[4,2,24,768]{3,2,1,0:T(8,128)(2,1)}), bf16[4,2,24,768]{3,2,1,0:T(8,128)(2,1)S(1)}, u32[]{:S(2)}, u32[]{:S(2)}) async-start(bf16[4,2,24,768]{3,2,1,0:T(8,128)(2,1)} %bitcast.18), calls=%async_computation.1 | async-start | bytes 589824 | tf_op jit(solution)/shard_map/all_to_all | solution.py:151
  26.9 0.0 copy-done
  26.9 9.9 %all-to-all-done.1 = bf16[4,2,24,768]{3,2,1,0:T(8,128)(2,1)S(1)} async-done(((bf16[4,2,24,768]{3,2,1,0:T(8,128)(2,1)}), bf16[4,2,24,768]{3,2,1,0:T(8,128)(2,1)S(1)}, u32[]{:S(2)}, u32[]{:S(2)}) %all-to-all-start.1) | async-done | bytes 294944 | tf_op jit(solution)/shard_map/all_to_all | solution.py:151
  36.8 5.1 %fusion.7 = f32[2,48,3072]{2,1,0:T(8,128)S(1)} fusion(bf16[2,2,48,768]{3,2,1,0:T(8,128)(2,1)S(1)} %bitcast.139, bf16[2,768,1536]{2,1,0:T(8,128)(2,1)} %bitcast.133, bf16[2,768,1536]{2,1,0:T(8,128)(2,1)} %bitcast.129), kind=kOutput, calls=%fused_computation.12 | convolution fusion | flops 924844032 | bytes 10911744 | tf_op jit(solution)/shard_map/dot_general | solution.py:61
  41.9 0.1 broadcast_multiply_fusion
  42.0 0.0 slice-done
  42.1 0.0 slice-done.1
  42.1 0.0 copy-start.3
  42.1 0.0 copy-start.2
  42.1 4.8 %fusion.13 = bf16[96,1536]{1,0:T(8,128)(2,1)S(1)} fusion(bf16[1536,1536]{1,0:T(8,128)(2,1)} %bitcast.134, bf16[1536,1536]{1,0:T(8,128)(2,1)S(1)} %bitcast.132, bf16[48,3072]{1,0:T(8,128)(2,1)S(1)} %get-tuple-element.5, bf16[48,3072]{1,0:T(8,128)(2,1)S(1)} %get-tuple-element.6), kind=kOutput, calls=%fused_computation.16 | convolution fusion | flops 926318592 | bytes 10321920 | tf_op jit(solution)/shard_map/dot_general | solution.py:50
  46.9 0.1 reshape.364
  47.0 0.7 %copy.10 = bf16[2,48,2,768]{3,1,2,0:T(8,128)(2,1)} copy(bf16[2,48,2,768]{3,2,1,0:T(2,128)(2,1)S(1)} %reshape.364) | data formatting | bytes 589824 | tf_op jit(solution)/shard_map/reshape | solution.py:72
  47.8 3.5 %all-to-all-start.2 = ((bf16[4,48,768]{2,1,0:T(8,128)(2,1)}), bf16[4,48,768]{2,1,0:T(8,128)(2,1)S(1)}, u32[]{:S(2)}, u32[]{:S(2)}) async-start(bf16[4,48,768]{2,1,0:T(8,128)(2,1)} %bitcast.32), calls=%async_computation.2 | async-start | bytes 589824 | tf_op jit(solution)/shard_map/all_to_all | solution.py:153
  51.2 8.1 %all-to-all-done.2 = bf16[4,48,768]{2,1,0:T(8,128)(2,1)S(1)} async-done(((bf16[4,48,768]{2,1,0:T(8,128)(2,1)}), bf16[4,48,768]{2,1,0:T(8,128)(2,1)S(1)}, u32[]{:S(2)}, u32[]{:S(2)}) %all-to-all-start.2) | async-done | bytes 294944 | tf_op jit(solution)/shard_map/all_to_all | solution.py:153
  59.3 0.1 fusion.47
  59.5 3.4 %collective-permute-start = (bf16[8,1,768]{2,1,0:T(2,128)(2,1)S(1)}, bf16[8,1,768]{2,1,0:T(2,128)(2,1)S(1)}, u32[]{:S(2)}, u32[]{:S(2)}) collective-permute-start(bf16[8,1,768]{2,1,0:T(2,128)(2,1)S(1)} %get-tuple-element.13), channel_id=1, source_target_pairs={{0,4},{4,8},{8,12},{1,5},{5,9},{9,13},{2,6},{6,10},{10,14},{3,7},{... | collective-permute-start | bytes 36872 | tf_op jit(solution)/shard_map/ppermute | solution.py:16
  62.9 1.3 %collective-permute-start.1 = (bf16[8,1,768]{2,1,0:T(2,128)(2,1)S(1)}, bf16[8,1,768]{2,1,0:T(2,128)(2,1)S(1)}, u32[]{:S(2)}, u32[]{:S(2)}) collective-permute-start(bf16[8,1,768]{2,1,0:T(2,128)(2,1)S(1)} %get-tuple-element.14), channel_id=1, source_target_pairs={{4,0},{8,4},{12,8},{5,1},{9,5},{13,9},{6,2},{10,6},{14,10},{7,3},{... | collective-permute-start | bytes 36872 | tf_op jit(solution)/shard_map/ppermute | solution.py:19
  64.2 0.0 copy-done.3
  64.2 0.2 collective-permute-done
  64.4 4.2 %collective-permute-done.1 = bf16[8,1,768]{2,1,0:T(2,128)(2,1)S(1)} collective-permute-done((bf16[8,1,768]{2,1,0:T(2,128)(2,1)S(1)}, bf16[8,1,768]{2,1,0:T(2,128)(2,1)S(1)}, u32[]{:S(2)}, u32[]{:S(2)}) %collective-permute-start.1) | collective-permute-done | bytes 12320 | tf_op jit(solution)/shard_map/ppermute | solution.py:19
  68.6 0.1 maximum_convert_fusion
  68.7 0.0 copy-done.2
  68.7 1.0 %fusion.25 = f32[1,8,24,768]{3,2,1,0:T(8,128)} fusion(f32[8,26,768]{2,1,0:T(8,128)S(1)} %maximum_convert_fusion, bf16[8,24,768]{2,1,0:T(8,128)(2,1)S(1)} %bitcast.137, f32[4,24,768]{2,1,0:T(8,128)S(1)} %get-tuple-element.12, f32[4,24,768]{2,1,0:T(8,128)S(1)} %bitcast_add_fusion, f32[24,768]{1,0:T(8,128)S(1)} %convert_select_fusion, f32[24,768]{1,0:T(8,128)S(1)} %bitcast.140), kind=kLoop, calls=%fused_computation.34 | loop fusion | flops 1327104 | bytes 2801664 | tf_op jit(solution)/shard_map/broadcast_in_dim | solution.py:157
  (19 shorter events, 0.4 us)
Async XLA Ops:
  0.0 26.9 %copy-start = (f32[1,8,3072]{2,1,0:T(8,128)S(1)}, f32[1,8,3072]{2,1,0:T(8,128)}, u32[]{:S(2)}) copy-start(f32[1,8,3072]{2,1,0:T(8,128)} %param.9) | copy-start | bytes 294916
  1.9 1.6 %copy-start.5 = (f32[1,1,1,16,128]{4,3,2,1,0:T(8,128)S(1)}, f32[1,1,1,16,128]{4,3,2,1,0:T(8,128)}, u32[]{:S(2)}) copy-start(f32[1,1,1,16,128]{4,3,2,1,0:T(8,128)} %param.14) | copy-start | bytes 24580
  1.9 1.6 %copy-start.6 = (s32[1,1,1,16]{3,2,1,0:T(1,128)S(1)}, s32[1,1,1,16]{3,2,1,0:T(1,128)}, u32[]{:S(2)}) copy-start(s32[1,1,1,16]{3,2,1,0:T(1,128)} %param.15) | copy-start | bytes 196
  1.9 11.4 %copy-start.4 = (s32[1,1,1,16,128]{4,3,2,1,0:T(8,128)S(1)}, s32[1,1,1,16,128]{4,3,2,1,0:T(8,128)}, u32[]{:S(2)}) copy-start(s32[1,1,1,16,128]{4,3,2,1,0:T(8,128)} %param.13) | copy-start | bytes 24580
  4.4 14.9 %all-to-all-start = ((f32[32,4,128]{2,1,0:T(4,128)}), f32[32,4,128]{2,1,0:T(4,128)S(1)}, u32[]{:S(2)}, u32[]{:S(2)}) async-start(f32[32,4,128]{2,1,0:T(4,128)} %maximum_select_fusion), calls=%async_computation | async-start | bytes 131072 | tf_op jit(solution)/shard_map/all_to_all | solution.py:144
  19.5 1.6 %copy-start.1 = (f32[1,8,24,768]{3,2,1,0:T(8,128)S(1)}, f32[1,8,24,768]{3,2,1,0:T(8,128)}, u32[]{:S(2)}) copy-start(f32[1,8,24,768]{3,2,1,0:T(8,128)} %param.8) | copy-start | bytes 1769476
  21.9 20.2 %slice-start = ((s8[4718592]{0:T(1024)(128)(4,1)}), s8[524288]{0:T(1024)(128)(4,1)S(1)}, s32[]{:S(2)}) async-start(s8[4718592]{0:T(1024)(128)(4,1)} %bitcast.130), calls=%async_computation.3 | async-start | bytes 1048576
  21.9 14.9 %all-to-all-start.1 = ((bf16[4,2,24,768]{3,2,1,0:T(8,128)(2,1)}), bf16[4,2,24,768]{3,2,1,0:T(8,128)(2,1)S(1)}, u32[]{:S(2)}, u32[]{:S(2)}) async-start(bf16[4,2,24,768]{3,2,1,0:T(8,128)(2,1)} %bitcast.18), calls=%async_computation.1 | async-start | bytes 589824 | tf_op jit(solution)/shard_map/all_to_all | solution.py:151
  36.8 5.2 %slice-start.1 = ((s8[4718592]{0:T(1024)(128)(4,1)}), s8[4194304]{0:T(1024)(128)(4,1)S(1)}, s32[]{:S(2)}) async-start(s8[4718592]{0:T(1024)(128)(4,1)} %bitcast.130), calls=%async_computation.4 | async-start | bytes 8388608
  42.1 22.1 %copy-start.3 = (s32[24,768]{1,0:T(8,128)S(1)}, s32[24,768]{1,0:T(8,128)}, u32[]{:S(2)}) copy-start(s32[24,768]{1,0:T(8,128)} %param.11) | copy-start | bytes 221188
  42.1 26.6 %copy-start.2 = (f32[1,24,768]{2,1,0:T(8,128)S(1)}, f32[1,24,768]{2,1,0:T(8,128)}, u32[]{:S(2)}) copy-start(f32[1,24,768]{2,1,0:T(8,128)} %param.10) | copy-start | bytes 221188
  47.8 11.6 %all-to-all-start.2 = ((bf16[4,48,768]{2,1,0:T(8,128)(2,1)}), bf16[4,48,768]{2,1,0:T(8,128)(2,1)S(1)}, u32[]{:S(2)}, u32[]{:S(2)}) async-start(bf16[4,48,768]{2,1,0:T(8,128)(2,1)} %bitcast.32), calls=%async_computation.2 | async-start | bytes 589824 | tf_op jit(solution)/shard_map/all_to_all | solution.py:153
  59.5 4.9 %collective-permute-start = (bf16[8,1,768]{2,1,0:T(2,128)(2,1)S(1)}, bf16[8,1,768]{2,1,0:T(2,128)(2,1)S(1)}, u32[]{:S(2)}, u32[]{:S(2)}) collective-permute-start(bf16[8,1,768]{2,1,0:T(2,128)(2,1)S(1)} %get-tuple-element.13), channel_id=1, source_target_pairs={{0,4},{4,8},{8,12},{1,5},{5,9},{9,13},{2,6},{6,10},{10,14},{3,7},{... | collective-permute-start | bytes 36872 | tf_op jit(solution)/shard_map/ppermute | solution.py:16
  62.9 5.7 %collective-permute-start.1 = (bf16[8,1,768]{2,1,0:T(2,128)(2,1)S(1)}, bf16[8,1,768]{2,1,0:T(2,128)(2,1)S(1)}, u32[]{:S(2)}, u32[]{:S(2)}) collective-permute-start(bf16[8,1,768]{2,1,0:T(2,128)(2,1)S(1)} %get-tuple-element.14), channel_id=1, source_target_pairs={{4,0},{8,4},{12,8},{5,1},{9,5},{13,9},{6,2},{10,6},{14,10},{7,3},{... | collective-permute-start | bytes 36872 | tf_op jit(solution)/shard_map/ppermute | solution.py:19

commit v6 on v5

--- a/solution.py
+++ b/solution.py
@@ -74,8 +74,14 @@
 
 
 def diffuse(fields, rate):
-    padded = extended(fields.astype(jnp.bfloat16), (("gx", 1),), 1).astype(fields.dtype)
-    return fields + rate[None] * (padded[:, 2:] + padded[:, :-2] - 2.0 * fields)
+    count = lax.axis_size("gx")
+    forward = [(i, i + 1) for i in range(count - 1)]
+    backward = [(target, source) for source, target in forward]
+    edge_low = lax.ppermute(fields[:, -1:].astype(jnp.bfloat16), "gx", forward)
+    edge_high = lax.ppermute(fields[:, :1].astype(jnp.bfloat16), "gx", backward)
+    above = jnp.concatenate([edge_low.astype(fields.dtype), fields[:, :-1]], axis=1)
+    below = jnp.concatenate([fields[:, 1:], edge_high.astype(fields.dtype)], axis=1)
+    return fields + rate[None] * (below + above - 2.0 * fields)
 
 
 def split3(values):

time: 70.2 us -> 70.3 us (level)
    mul x0 -> x1, other arithmetic: none -> 1.06 us  [local(): fields = diffuse(fields, rate) * keep[None]]
    broadcast_in_dim x1 -> x0, other arithmetic: 1.02 us -> none  [local(): return fields[None]]
    another operation x1 -> x2, other arithmetic: 5.22 us -> 5.32 us
where the time goes in v6:
time: 70.3 us; the launch traced here: 69.8 us
  waiting for transfers between devices  22.4 us (32%)
  starting transfers between devices  20.5 us (29%)
  matrix products  12.6 us (18%)
  other arithmetic  11.9 us (17%)
  local copies, waits for them, and re-layouts  2.03 us (3%)
    all_to_all x1, waiting for transfers between devices, local(): lax.all_to_all(grid_bf, 'gy', split_axis=0, concat_axis=0, tiled=True)  9.87 us
    all_to_all x1, waiting for transfers between devices, local(): incr = lax.all_to_all(incr, 'gy', split_axis=0, concat_axis=0, tiled=True)  8.09 us
    all_to_all x1, starting transfers between devices, local(): lax.all_to_all(spread, ('comp', 'gx', 'gy'), split_axis=0, concat_axis=0,...  7.32 us
    another operation x2, other arithmetic  5.32 us
    dot_general x1, matrix products, circle_increment(): lax.dot_general(grid, table.reshape(parts // 2, cols_dev, cols_all), (((1...  5.1 us
    all_to_all x1, starting transfers between devices, local(): lax.all_to_all(grid_bf, 'gy', split_axis=0, concat_axis=0, tiled=True)  5.02 us
    dot_general x1, matrix products, back_transform(): lax.dot_general(filtered, table_part, (((1,), (1,)), ((), ())), preferred...  4.82 us
    ppermute x1, waiting for transfers between devices, diffuse(): edge_high = lax.ppermute(fields[:, :1].astype(jnp.bfloat16), 'gx', backward)  4.28 us
  transfers between devices with their start and end apart: 5, of which 4 were waited for; matrix products, arithmetic and copies ran while one was open for 11% of the time, Pallas kernels for 0%

profile of v6, /device:TPU:0, one launch (start us, length us, event | category | flops | bytes accessed | tf_op | source)
XLA Modules:
  0.0 69.8 jit_solution(5301875344611813317)
XLA Ops:
  0.0 0.0 copy-start
  0.0 1.0 %slice.50 = f32[1,4,24,768]{3,2,1,0:T(8,128)S(1)} slice(f32[1,8,24,768]{3,2,1,0:T(8,128)} %param.8), slice={[0:1], [0:4], [0:24], [0:768]} | slice | bytes 589824 | tf_op jit(solution)/shard_map/slice | solution.py:143
  1.1 0.7 %add_select_fusion.5 = (s32[2048]{0:T(1024)S(1)}, s32[2048]{0:T(1024)S(1)}) fusion(s32[1,1,1,16,128]{4,3,2,1,0:T(8,128)} %param.12), kind=kLoop, calls=%fused_computation.98 | loop fusion | flops 24576 | bytes 24576 | tf_op jit(solution)/shard_map/jit(floor_divide)/jit(_where)/select_n | solution.py:103
  1.8 0.0 copy-start.5
  1.8 0.0 copy-start.6
  1.8 0.0 copy-start.4
  1.8 1.2 %fusion.5 = f32[288,2048]{1,0:T(8,128)S(1)} fusion(s32[2048]{0:T(1024)S(1)} %get-tuple-element.25, bf16[96,768]{1,0:T(8,128)(2,1)S(1)} %get-tuple-element.21, bf16[96,768]{1,0:T(8,128)(2,1)S(1)} %get-tuple-element.20, bf16[96,768]{1,0:T(8,128)(2,1)S(1)} %bitcast_convert_fusion.1), kind=kOutput, calls=%fused_computation.10 | convolution fusion | flops 908869632 | bytes 2809856 | tf_op jit(solution)/shard_map/dot_general | solution.py:97
  3.1 0.1 slice_add_fusion
  3.3 0.1 select_reduce_fusion
  3.4 0.0 copy-done.5
  3.4 0.0 copy-done.6
  3.4 0.1 bitcast_select_fusion
  3.5 0.7 %maximum_select_fusion = f32[32,4,128]{2,1,0:T(4,128)} fusion(f32[16,4,128]{2,1,0:T(4,128)S(1)} %fusion.55, pred[32]{0:T(512)(128)(4,1)S(1)} %fusion.68), kind=kLoop, calls=%fused_computation.84 | loop fusion | flops 32768 | bytes 98336 | tf_op jit(solution)/shard_map/jit(_where)/select_n | solution.py:149
  4.3 7.3 %all-to-all-start = ((f32[32,4,128]{2,1,0:T(4,128)}), f32[32,4,128]{2,1,0:T(4,128)S(1)}, u32[]{:S(2)}, u32[]{:S(2)}) async-start(f32[32,4,128]{2,1,0:T(4,128)} %maximum_select_fusion), calls=%async_computation | async-start | bytes 131072 | tf_op jit(solution)/shard_map/all_to_all | solution.py:150
  11.6 1.6 %fusion.44 = (f32[64,1536]{1,0:T(8,128)S(1)}, f32[64,1536]{1,0:T(8,128)S(1)}) fusion(), kind=kLoop, calls=%fused_computation.60 | loop fusion | flops 884736 | bytes 786432 | tf_op jit(solution)/shard_map/sin | solution.py:37
  13.2 0.0 copy-done.4
  13.2 0.7 fusion.53
  13.9 5.2 %subtract_convert_fusion = (bf16[24,64,1536]{2,1,0:T(8,128)(2,1)}, bf16[24,64,1536]{2,1,0:T(8,128)(2,1)}) fusion(f32[64,1536]{1,0:T(8,128)S(1)} %get-tuple-element.28, f32[24,1536]{1,0:T(8,128)S(1)} %get-tuple-element.27, f32[64,1536]{1,0:T(8,128)S(1)} %get-tuple-element.29, f32[24,1536]{1,0:T(8,128)S(1)} %get-tuple-element.26), kind=kLoop, calls=%fused_computation.6 | loop fusion | flops 18874368 | bytes 10518528 | tf_op jit(solution)/shard_map/convert.13
  19.2 0.0 all-to-all-done
  19.2 0.1 broadcast_select_fusion
  19.3 0.1 fusion.32
  19.4 0.0 copy-start.1
  19.4 1.5 %fusion.6 = f32[288,768]{1,0:T(8,128)S(1)} fusion(s32[2048]{0:T(1024)S(1)} %get-tuple-element.23, bf16[96,2048]{1,0:T(8,128)(2,1)S(1)} %get-tuple-element.12, bf16[96,2048]{1,0:T(8,128)(2,1)S(1)} %get-tuple-element.11, bf16[96,2048]{1,0:T(8,128)(2,1)S(1)} %bitcast_convert_fusion), kind=kOutput, calls=%fused_computation.11 | convolution fusion | flops 911081472 | bytes 2072576 | tf_op jit(solution)/shard_map/dot_general | solution.py:97
  21.0 0.0 copy-done.1
  21.0 0.1 slice_add_fusion.4
  21.1 0.7 %fusion.34 = bf16[8,24,768]{2,1,0:T(8,128)(2,1)} fusion(f32[4,24,768]{2,1,0:T(8,128)S(1)} %get-tuple-element.14, f32[4,24,768]{2,1,0:T(8,128)S(1)} %bitcast_add_fusion), kind=kLoop, calls=%fused_computation.49 | loop fusion | flops 147456 | bytes 884736 | tf_op jit(solution)/shard_map/convert_element_type | solution.py:155
  21.9 5.0 %all-to-all-start.1 = ((bf16[4,2,24,768]{3,2,1,0:T(8,128)(2,1)}), bf16[4,2,24,768]{3,2,1,0:T(8,128)(2,1)S(1)}, u32[]{:S(2)}, u32[]{:S(2)}) async-start(bf16[4,2,24,768]{3,2,1,0:T(8,128)(2,1)} %bitcast.19), calls=%async_computation.1 | async-start | bytes 589824 | tf_op jit(solution)/shard_map/all_to_all | solution.py:157
  26.9 0.0 copy-done
  26.9 9.9 %all-to-all-done.1 = bf16[4,2,24,768]{3,2,1,0:T(8,128)(2,1)S(1)} async-done(((bf16[4,2,24,768]{3,2,1,0:T(8,128)(2,1)}), bf16[4,2,24,768]{3,2,1,0:T(8,128)(2,1)S(1)}, u32[]{:S(2)}, u32[]{:S(2)}) %all-to-all-start.1) | async-done | bytes 294944 | tf_op jit(solution)/shard_map/all_to_all | solution.py:157
  36.8 5.1 %fusion.7 = f32[2,48,3072]{2,1,0:T(8,128)S(1)} fusion(bf16[2,2,48,768]{3,2,1,0:T(8,128)(2,1)S(1)} %bitcast.149, bf16[2,768,1536]{2,1,0:T(8,128)(2,1)} %bitcast.144, bf16[2,768,1536]{2,1,0:T(8,128)(2,1)} %bitcast.140), kind=kOutput, calls=%fused_computation.12 | convolution fusion | flops 924844032 | bytes 10911744 | tf_op jit(solution)/shard_map/dot_general | solution.py:61
  41.9 0.1 broadcast_multiply_fusion
  42.0 0.0 slice-done
  42.1 0.0 copy-start.3
  42.1 4.8 %fusion.13 = bf16[96,1536]{1,0:T(8,128)(2,1)S(1)} fusion(bf16[1536,1536]{1,0:T(8,128)(2,1)} %bitcast.145, bf16[1536,1536]{1,0:T(8,128)(2,1)S(1)} %bitcast.143, bf16[48,3072]{1,0:T(8,128)(2,1)S(1)} %get-tuple-element.7, bf16[48,3072]{1,0:T(8,128)(2,1)S(1)} %get-tuple-element.8), kind=kOutput, calls=%fused_computation.16 | convolution fusion | flops 926318592 | bytes 10321920 | tf_op jit(solution)/shard_map/dot_general | solution.py:50
  46.9 0.0 copy-start.2
  46.9 0.1 reshape.476
  47.0 0.7 %copy.10 = bf16[2,48,2,768]{3,1,2,0:T(8,128)(2,1)} copy(bf16[2,48,2,768]{3,2,1,0:T(2,128)(2,1)S(1)} %reshape.476) | data formatting | bytes 589824 | tf_op jit(solution)/shard_map/reshape | solution.py:72
  47.7 3.5 %all-to-all-start.2 = ((bf16[4,48,768]{2,1,0:T(8,128)(2,1)}), bf16[4,48,768]{2,1,0:T(8,128)(2,1)S(1)}, u32[]{:S(2)}, u32[]{:S(2)}) async-start(bf16[4,48,768]{2,1,0:T(8,128)(2,1)} %bitcast.33), calls=%async_computation.2 | async-start | bytes 589824 | tf_op jit(solution)/shard_map/all_to_all | solution.py:159
  51.2 0.0 copy-done.3
  51.2 8.1 %all-to-all-done.2 = bf16[4,48,768]{2,1,0:T(8,128)(2,1)S(1)} async-done(((bf16[4,48,768]{2,1,0:T(8,128)(2,1)}), bf16[4,48,768]{2,1,0:T(8,128)(2,1)S(1)}, u32[]{:S(2)}, u32[]{:S(2)}) %all-to-all-start.2) | async-done | bytes 294944 | tf_op jit(solution)/shard_map/all_to_all | solution.py:159
  59.4 0.1 fusion.73
  59.5 3.4 %collective-permute-start.1 = (bf16[8,1,768]{2,1,0:T(2,128)(2,1)S(1)}, bf16[8,1,768]{2,1,0:T(2,128)(2,1)S(1)}, u32[]{:S(2)}, u32[]{:S(2)}) collective-permute-start(bf16[8,1,768]{2,1,0:T(2,128)(2,1)S(1)} %get-tuple-element.18), channel_id=1, source_target_pairs={{0,4},{4,8},{8,12},{1,5},{5,9},{9,13},{2,6},{6,10},{10,14},{3,7},{... | collective-permute-start | bytes 36872 | tf_op jit(solution)/shard_map/ppermute | solution.py:80
  62.9 0.1 slice_bitcast_fusion
  63.0 1.3 %collective-permute-start = (bf16[8,1,768]{2,1,0:T(2,128)(2,1)S(1)}, bf16[8,1,768]{2,1,0:T(2,128)(2,1)S(1)}, u32[]{:S(2)}, u32[]{:S(2)}) collective-permute-start(bf16[8,1,768]{2,1,0:T(2,128)(2,1)S(1)} %get-tuple-element.19), channel_id=1, source_target_pairs={{4,0},{8,4},{12,8},{5,1},{9,5},{13,9},{6,2},{10,6},{14,10},{7,3},{... | collective-permute-start | bytes 36872 | tf_op jit(solution)/shard_map/ppermute | solution.py:81
  64.3 0.1 collective-permute-done.1
  64.4 4.3 %collective-permute-done = bf16[8,1,768]{2,1,0:T(2,128)(2,1)S(1)} collective-permute-done((bf16[8,1,768]{2,1,0:T(2,128)(2,1)S(1)}, bf16[8,1,768]{2,1,0:T(2,128)(2,1)S(1)}, u32[]{:S(2)}, u32[]{:S(2)}) %collective-permute-start) | collective-permute-done | bytes 12320 | tf_op jit(solution)/shard_map/ppermute | solution.py:81
  68.7 0.0 copy-done.2
  68.8 1.1 %fusion.31 = f32[1,8,24,768]{3,2,1,0:T(8,128)} fusion(f32[1,8,1,768]{3,2,1,0:T(1,128)S(1)} %bitcast_convert_fusion.3, f32[1,8,23,768]{3,2,1,0:T(8,128)S(1)} %get-tuple-element.17, f32[1,8,23,768]{3,2,1,0:T(8,128)S(1)} %get-tuple-element.16, f32[1,8,1,768]{3,2,1,0:T(1,128)S(1)} %bitcast_convert_fusion.2, f32[1,8,24,768]{3,2,1,0:T(8,128)S(1)} %bitcast.139, ...), kind=kLoop, calls=%fused_computation.46 | loop fusion | flops 1474560 | bytes 3096576 | tf_op jit(solution)/shard_map/mul | solution.py:162
  (23 shorter events, 0.5 us)
Async XLA Ops:
  0.0 26.9 %copy-start = (f32[1,8,3072]{2,1,0:T(8,128)S(1)}, f32[1,8,3072]{2,1,0:T(8,128)}, u32[]{:S(2)}) copy-start(f32[1,8,3072]{2,1,0:T(8,128)} %param.9) | copy-start | bytes 294916
  1.8 1.6 %copy-start.5 = (f32[1,1,1,16,128]{4,3,2,1,0:T(8,128)S(1)}, f32[1,1,1,16,128]{4,3,2,1,0:T(8,128)}, u32[]{:S(2)}) copy-start(f32[1,1,1,16,128]{4,3,2,1,0:T(8,128)} %param.14) | copy-start | bytes 24580
  1.8 1.6 %copy-start.6 = (s32[1,1,1,16]{3,2,1,0:T(1,128)S(1)}, s32[1,1,1,16]{3,2,1,0:T(1,128)}, u32[]{:S(2)}) copy-start(s32[1,1,1,16]{3,2,1,0:T(1,128)} %param.15) | copy-start | bytes 196
  1.8 11.4 %copy-start.4 = (s32[1,1,1,16,128]{4,3,2,1,0:T(8,128)S(1)}, s32[1,1,1,16,128]{4,3,2,1,0:T(8,128)}, u32[]{:S(2)}) copy-start(s32[1,1,1,16,128]{4,3,2,1,0:T(8,128)} %param.13) | copy-start | bytes 24580
  4.3 14.9 %all-to-all-start = ((f32[32,4,128]{2,1,0:T(4,128)}), f32[32,4,128]{2,1,0:T(4,128)S(1)}, u32[]{:S(2)}, u32[]{:S(2)}) async-start(f32[32,4,128]{2,1,0:T(4,128)} %maximum_select_fusion), calls=%async_computation | async-start | bytes 131072 | tf_op jit(solution)/shard_map/all_to_all | solution.py:150
  19.4 1.6 %copy-start.1 = (f32[1,8,24,768]{3,2,1,0:T(8,128)S(1)}, f32[1,8,24,768]{3,2,1,0:T(8,128)}, u32[]{:S(2)}) copy-start(f32[1,8,24,768]{3,2,1,0:T(8,128)} %param.8) | copy-start | bytes 1769476
  21.9 20.2 %slice-start = ((s8[4718592]{0:T(1024)(128)(4,1)}), s8[524288]{0:T(1024)(128)(4,1)S(1)}, s32[]{:S(2)}) async-start(s8[4718592]{0:T(1024)(128)(4,1)} %bitcast.141), calls=%async_computation.3 | async-start | bytes 1048576
  21.9 14.9 %all-to-all-start.1 = ((bf16[4,2,24,768]{3,2,1,0:T(8,128)(2,1)}), bf16[4,2,24,768]{3,2,1,0:T(8,128)(2,1)S(1)}, u32[]{:S(2)}, u32[]{:S(2)}) async-start(bf16[4,2,24,768]{3,2,1,0:T(8,128)(2,1)} %bitcast.19), calls=%async_computation.1 | async-start | bytes 589824 | tf_op jit(solution)/shard_map/all_to_all | solution.py:157
  36.8 5.3 %slice-start.1 = ((s8[4718592]{0:T(1024)(128)(4,1)}), s8[4194304]{0:T(1024)(128)(4,1)S(1)}, s32[]{:S(2)}) async-start(s8[4718592]{0:T(1024)(128)(4,1)} %bitcast.141), calls=%async_computation.4 | async-start | bytes 8388608
  42.1 9.1 %copy-start.3 = (s32[24,768]{1,0:T(8,128)S(1)}, s32[24,768]{1,0:T(8,128)}, u32[]{:S(2)}) copy-start(s32[24,768]{1,0:T(8,128)} %param.11) | copy-start | bytes 221188
  46.9 21.8 %copy-start.2 = (f32[1,24,768]{2,1,0:T(8,128)S(1)}, f32[1,24,768]{2,1,0:T(8,128)}, u32[]{:S(2)}) copy-start(f32[1,24,768]{2,1,0:T(8,128)} %param.10) | copy-start | bytes 221188
  47.7 11.6 %all-to-all-start.2 = ((bf16[4,48,768]{2,1,0:T(8,128)(2,1)}), bf16[4,48,768]{2,1,0:T(8,128)(2,1)S(1)}, u32[]{:S(2)}, u32[]{:S(2)}) async-start(bf16[4,48,768]{2,1,0:T(8,128)(2,1)} %bitcast.33), calls=%async_computation.2 | async-start | bytes 589824 | tf_op jit(solution)/shard_map/all_to_all | solution.py:159
  59.5 4.9 %collective-permute-start.1 = (bf16[8,1,768]{2,1,0:T(2,128)(2,1)S(1)}, bf16[8,1,768]{2,1,0:T(2,128)(2,1)S(1)}, u32[]{:S(2)}, u32[]{:S(2)}) collective-permute-start(bf16[8,1,768]{2,1,0:T(2,128)(2,1)S(1)} %get-tuple-element.18), channel_id=1, source_target_pairs={{0,4},{4,8},{8,12},{1,5},{5,9},{9,13},{2,6},{6,10},{10,14},{3,7},{... | collective-permute-start | bytes 36872 | tf_op jit(solution)/shard_map/ppermute | solution.py:80
  63.0 5.7 %collective-permute-start = (bf16[8,1,768]{2,1,0:T(2,128)(2,1)S(1)}, bf16[8,1,768]{2,1,0:T(2,128)(2,1)S(1)}, u32[]{:S(2)}, u32[]{:S(2)}) collective-permute-start(bf16[8,1,768]{2,1,0:T(2,128)(2,1)S(1)} %get-tuple-element.19), channel_id=1, source_target_pairs={{4,0},{8,4},{12,8},{5,1},{9,5},{13,9},{6,2},{10,6},{14,10},{7,3},{... | collective-permute-start | bytes 36872 | tf_op jit(solution)/shard_map/ppermute | solution.py:81
